TPU v7x, 256 devices: a whole 4x4x8 slice. The times are simulated.
256 devices in a mesh: gx: 32 (over x, z), gy: 8 (over y, core).
Axes of the slice: x: 4, y: 4, z: 8, core: 2. Of those that a mesh axis runs over, the one named last changes fastest.
Arguments:
- flow_state: float32 [4, 4096, 1024], P(None, 'gx', 'gy'), may hold values from -6 to 6
- sound_speed_sq: float32 [4096, 1024], P('gx', 'gy'), may hold values from 0.25 to 1
- snapshots: bfloat16 [62, 4096, 1024], P(None, 'gx', 'gy'), may hold values from -96 to 96
Outputs:
- new_state: float32 [4, 4096, 1024], P(None, 'gx', 'gy')
- pod_basis: float32 [64, 4096, 1024], P(None, 'gx', 'gy')
All inputs are finite; a program needn't handle non-finite values.
Results may differ from a plain program's by a relative error of at most 0.00063.
Values sent between devices are 32-bit elements; how exact they have to be, the bound alone decides.
A program may use at most 64 MiB of HBM per device.

v0:
```python
import jax
import jax.numpy as jnp
from jax import lax
from jax.sharding import PartitionSpec as P

STEPS = 2


courant = 0.8
stream_speed = 0.3
span_speed = 0.1


def padded_2(block, sides, width):
    for axis, dim in sides:
        count = lax.axis_size(axis)
        forward = [(i, i + 1) for i in range(count - 1)]
        forward.append((count - 1, 0))
        backward = [(target, source) for source, target in forward]
        low = lax.ppermute(
            lax.slice_in_dim(block, block.shape[dim] - width, None, axis=dim), axis, forward
        )
        high = lax.ppermute(lax.slice_in_dim(block, 0, width, axis=dim), axis, backward)
        block = jnp.concatenate([low, block, high], axis=dim)
    return block


def derivative_x(padded):
    interior = padded[:, :, 2:-2]
    extent = interior.shape[1] - 4
    ahead_one = interior[:, 3 : 3 + extent]
    behind_one = interior[:, 1 : 1 + extent]
    ahead_two = interior[:, 4 : 4 + extent]
    behind_two = interior[:, 0:extent]
    return (8.0 * (ahead_one - behind_one) - (ahead_two - behind_two)) / 12.0


def derivative_y(padded):
    interior = padded[:, 2:-2, :]
    extent = interior.shape[2] - 4
    ahead_one = interior[:, :, 3 : 3 + extent]
    behind_one = interior[:, :, 1 : 1 + extent]
    ahead_two = interior[:, :, 4 : 4 + extent]
    behind_two = interior[:, :, 0:extent]
    return (8.0 * (ahead_one - behind_one) - (ahead_two - behind_two)) / 12.0


def tendency(padded, sound_sq):
    slope_x = derivative_x(padded)
    slope_y = derivative_y(padded)
    advect = stream_speed * slope_x + span_speed * slope_y
    diverge = slope_x[1] + slope_y[2]
    rate_rho = -courant * (advect[0] + diverge)
    rate_mx = -courant * (advect[1] + slope_x[3])
    rate_my = -courant * (advect[2] + slope_y[3])
    rate_p = -courant * (advect[3] + sound_sq * diverge)
    return jnp.stack([rate_rho, rate_mx, rate_my, rate_p])


def extend(current):
    return padded_2(current, (("gx", 1), ("gy", 2)), 2)


def advance(current, sound_sq):
    first = current + tendency(extend(current), sound_sq)
    second = 0.75 * current + 0.25 * (first + tendency(extend(first), sound_sq))
    return 1.0 / 3.0 * current + 2.0 / 3.0 * (second + tendency(extend(second), sound_sq))


def body(flow_state, sound_speed_sq, snapshots):
    current = flow_state
    columns = [snapshots]
    for step_index in range(STEPS):
        current = advance(current, sound_speed_sq)
        columns.append(current[3].astype(jnp.bfloat16)[None])
    snap_block = jnp.concatenate(columns, axis=0)
    mode_count = snap_block.shape[0]
    flat_block = snap_block.reshape(mode_count, -1)
    cell_total = flat_block.shape[1] * lax.axis_size("gx") * lax.axis_size("gy")
    local_gram = (
        lax.dot_general(
            flat_block, flat_block, (((1,), (1,)), ((), ())), preferred_element_type=jnp.float32
        )
        / cell_total
    )
    gram = lax.psum(local_gram, ("gx", "gy"))
    lower_factor = jnp.linalg.cholesky(gram)
    identity_matrix = jnp.eye(mode_count, dtype=jnp.float32)
    inverse = jax.scipy.linalg.solve_triangular(lower_factor, identity_matrix, lower=True)
    pod_basis = jnp.dot(inverse, flat_block.astype(jnp.float32), precision=lax.Precision.HIGHEST)
    return (current, pod_basis.reshape(snap_block.shape))


def solution(mesh):
    placed = (P(None, "gx", "gy"), P("gx", "gy"), P(None, "gx", "gy"))
    return jax.shard_map(
        body,
        mesh=mesh,
        in_specs=placed,
        out_specs=(P(None, "gx", "gy"), P(None, "gx", "gy")),
        check_vma=False,
    )
```

profile of v0, /device:TPU:1, one launch (start us, length us, event | category | flops | bytes accessed | tf_op | source)
XLA Modules:
  0.0 197.1 jit_solution(15976753331273612163)
XLA Ops:
  1.4 2.5 %collective-permute-start.1 = (f32[4,2,128]{2,1,0:T(2,128)S(1)}, f32[4,2,128]{2,1,0:T(2,128)S(1)}, u32[]{:S(2)}, u32[]{:S(2)}) collective-permute-start(f32[4,2,128]{2,1,0:T(2,128)S(1)} %get-tuple-element.73), channel_id=1, source_target_pairs={{0,8},{8,16},{16,24},{24,32},{32,40},{40,48},{48,56},{56,64},{64,7... | collective-permute-start | bytes 12296 | tf_op jit(solution)/shard_map/ppermute | solution.py:20
  3.9 6.2 %collective-permute-start = (f32[4,2,128]{2,1,0:T(2,128)S(1)}, f32[4,2,128]{2,1,0:T(2,128)S(1)}, u32[]{:S(2)}, u32[]{:S(2)}) collective-permute-start(f32[4,2,128]{2,1,0:T(2,128)S(1)} %get-tuple-element.74), channel_id=1, source_target_pairs={{8,0},{16,8},{24,16},{32,24},{40,32},{48,40},{56,48},{64,56},{72,6... | collective-permute-start | bytes 12296 | tf_op jit(solution)/shard_map/ppermute | solution.py:23
  14.9 4.5 %collective-permute-done.2 = f32[4,132,2]{2,1,0:T(8,128)S(1)} collective-permute-done((f32[4,132,2]{2,1,0:T(8,128)S(1)}, f32[4,132,2]{2,1,0:T(8,128)S(1)}, u32[]{:S(2)}, u32[]{:S(2)}) %collective-permute-start.2) | collective-permute-done | bytes 4256 | tf_op jit(solution)/shard_map/ppermute | solution.py:23
  19.4 2.0 %broadcast_multiply_fusion.10 = (f32[4,128,128]{2,1,0:T(8,128)S(1)}, f32[4,128,128]{2,1,0:T(8,128)S(1)}, f32[4,130,128]{2,1,0:T(8,128)S(1)}) fusion(f32[4,2,128]{2,1,0:T(2,128)S(1)} %collective-permute-done, f32[4,128,128]{2,1,0:T(8,128)} %param.3, f32[4,2,128]{2,1,0:T(2,128)S(1)} %collective-permute-done.1, f32[4,132,2]{2,1,0:T(8,128)S(1)} %collective-permute-done.3, ...), kind=kLoop, calls=%fused_computation.177 | loop fusion | flops 1114111 | bytes 1065216 | tf_op jit(solution)/shard_map/div | solution.py:45
  21.8 5.2 %collective-permute-start.4 = (f32[4,2,128]{2,1,0:T(2,128)S(1)}, f32[4,2,128]{2,1,0:T(2,128)S(1)}, u32[]{:S(2)}, u32[]{:S(2)}) collective-permute-start(f32[4,2,128]{2,1,0:T(2,128)S(1)} %get-tuple-element.71), channel_id=1, source_target_pairs={{8,0},{16,8},{24,16},{32,24},{40,32},{48,40},{56,48},{64,56},{72,6... | collective-permute-start | bytes 12296 | tf_op jit(solution)/shard_map/ppermute | solution.py:23
  28.1 3.9 %collective-permute-start.6 = (f32[4,132,2]{2,1,0:T(8,128)S(1)}, f32[4,132,2]{2,1,0:T(8,128)S(1)}, u32[]{:S(2)}, u32[]{:S(2)}) collective-permute-start(f32[4,132,2]{2,1,0:T(8,128)S(1)} %get-tuple-element.58), channel_id=1, source_target_pairs={{1,0},{2,1},{3,2},{4,3},{5,4},{6,5},{7,6},{0,7},{9,8},{10,9},{11,1... | collective-permute-start | bytes 12680 | tf_op jit(solution)/shard_map/ppermute | solution.py:23
  32.1 2.6 %collective-permute-done.6 = f32[4,132,2]{2,1,0:T(8,128)S(1)} collective-permute-done((f32[4,132,2]{2,1,0:T(8,128)S(1)}, f32[4,132,2]{2,1,0:T(8,128)S(1)}, u32[]{:S(2)}, u32[]{:S(2)}) %collective-permute-start.6) | collective-permute-done | bytes 4256 | tf_op jit(solution)/shard_map/ppermute | solution.py:23
  36.3 5.1 %collective-permute-start.8 = (f32[4,2,128]{2,1,0:T(2,128)S(1)}, f32[4,2,128]{2,1,0:T(2,128)S(1)}, u32[]{:S(2)}, u32[]{:S(2)}) collective-permute-start(f32[4,2,128]{2,1,0:T(2,128)S(1)} %get-tuple-element.69), channel_id=1, source_target_pairs={{8,0},{16,8},{24,16},{32,24},{40,32},{48,40},{56,48},{64,56},{72,6... | collective-permute-start | bytes 12296 | tf_op jit(solution)/shard_map/ppermute | solution.py:23
  42.6 4.6 %collective-permute-start.10 = (f32[4,132,2]{2,1,0:T(8,128)S(1)}, f32[4,132,2]{2,1,0:T(8,128)S(1)}, u32[]{:S(2)}, u32[]{:S(2)}) collective-permute-start(f32[4,132,2]{2,1,0:T(8,128)S(1)} %get-tuple-element.56), channel_id=1, source_target_pairs={{1,0},{2,1},{3,2},{4,3},{5,4},{6,5},{7,6},{0,7},{9,8},{10,9},{11,1... | collective-permute-start | bytes 12680 | tf_op jit(solution)/shard_map/ppermute | solution.py:23
  47.3 2.9 %collective-permute-done.10 = f32[4,132,2]{2,1,0:T(8,128)S(1)} collective-permute-done((f32[4,132,2]{2,1,0:T(8,128)S(1)}, f32[4,132,2]{2,1,0:T(8,128)S(1)}, u32[]{:S(2)}, u32[]{:S(2)}) %collective-permute-start.10) | collective-permute-done | bytes 4256 | tf_op jit(solution)/shard_map/ppermute | solution.py:23
  51.5 5.2 %collective-permute-start.12 = (f32[4,2,128]{2,1,0:T(2,128)S(1)}, f32[4,2,128]{2,1,0:T(2,128)S(1)}, u32[]{:S(2)}, u32[]{:S(2)}) collective-permute-start(f32[4,2,128]{2,1,0:T(2,128)S(1)} %get-tuple-element.67), channel_id=1, source_target_pairs={{8,0},{16,8},{24,16},{32,24},{40,32},{48,40},{56,48},{64,56},{72,6... | collective-permute-start | bytes 12296 | tf_op jit(solution)/shard_map/ppermute | solution.py:23
  57.9 4.6 %collective-permute-start.14 = (f32[4,132,2]{2,1,0:T(8,128)S(1)}, f32[4,132,2]{2,1,0:T(8,128)S(1)}, u32[]{:S(2)}, u32[]{:S(2)}) collective-permute-start(f32[4,132,2]{2,1,0:T(8,128)S(1)} %get-tuple-element.54), channel_id=1, source_target_pairs={{1,0},{2,1},{3,2},{4,3},{5,4},{6,5},{7,6},{0,7},{9,8},{10,9},{11,1... | collective-permute-start | bytes 12680 | tf_op jit(solution)/shard_map/ppermute | solution.py:23
  62.6 2.9 %collective-permute-done.14 = f32[4,132,2]{2,1,0:T(8,128)S(1)} collective-permute-done((f32[4,132,2]{2,1,0:T(8,128)S(1)}, f32[4,132,2]{2,1,0:T(8,128)S(1)}, u32[]{:S(2)}, u32[]{:S(2)}) %collective-permute-start.14) | collective-permute-done | bytes 4256 | tf_op jit(solution)/shard_map/ppermute | solution.py:23
  66.8 5.4 %collective-permute-start.16 = (f32[4,2,128]{2,1,0:T(2,128)S(1)}, f32[4,2,128]{2,1,0:T(2,128)S(1)}, u32[]{:S(2)}, u32[]{:S(2)}) collective-permute-start(f32[4,2,128]{2,1,0:T(2,128)S(1)} %get-tuple-element.65), channel_id=1, source_target_pairs={{8,0},{16,8},{24,16},{32,24},{40,32},{48,40},{56,48},{64,56},{72,6... | collective-permute-start | bytes 12296 | tf_op jit(solution)/shard_map/ppermute | solution.py:23
  75.4 4.0 %collective-permute-start.18 = (f32[4,132,2]{2,1,0:T(8,128)S(1)}, f32[4,132,2]{2,1,0:T(8,128)S(1)}, u32[]{:S(2)}, u32[]{:S(2)}) collective-permute-start(f32[4,132,2]{2,1,0:T(8,128)S(1)} %get-tuple-element.52), channel_id=1, source_target_pairs={{1,0},{2,1},{3,2},{4,3},{5,4},{6,5},{7,6},{0,7},{9,8},{10,9},{11,1... | collective-permute-start | bytes 12680 | tf_op jit(solution)/shard_map/ppermute | solution.py:23
  79.5 2.9 %collective-permute-done.18 = f32[4,132,2]{2,1,0:T(8,128)S(1)} collective-permute-done((f32[4,132,2]{2,1,0:T(8,128)S(1)}, f32[4,132,2]{2,1,0:T(8,128)S(1)}, u32[]{:S(2)}, u32[]{:S(2)}) %collective-permute-start.18) | collective-permute-done | bytes 4256 | tf_op jit(solution)/shard_map/ppermute | solution.py:23
  83.7 4.8 %collective-permute-start.20 = (f32[4,2,128]{2,1,0:T(2,128)S(1)}, f32[4,2,128]{2,1,0:T(2,128)S(1)}, u32[]{:S(2)}, u32[]{:S(2)}) collective-permute-start(f32[4,2,128]{2,1,0:T(2,128)S(1)} %get-tuple-element.63), channel_id=1, source_target_pairs={{8,0},{16,8},{24,16},{32,24},{40,32},{48,40},{56,48},{64,56},{72,6... | collective-permute-start | bytes 12296 | tf_op jit(solution)/shard_map/ppermute | solution.py:23
  89.7 4.9 %collective-permute-start.22 = (f32[4,132,2]{2,1,0:T(8,128)S(1)}, f32[4,132,2]{2,1,0:T(8,128)S(1)}, u32[]{:S(2)}, u32[]{:S(2)}) collective-permute-start(f32[4,132,2]{2,1,0:T(8,128)S(1)} %get-tuple-element.50), channel_id=1, source_target_pairs={{1,0},{2,1},{3,2},{4,3},{5,4},{6,5},{7,6},{0,7},{9,8},{10,9},{11,1... | collective-permute-start | bytes 12680 | tf_op jit(solution)/shard_map/ppermute | solution.py:23
  94.7 2.9 %collective-permute-done.22 = f32[4,132,2]{2,1,0:T(8,128)S(1)} collective-permute-done((f32[4,132,2]{2,1,0:T(8,128)S(1)}, f32[4,132,2]{2,1,0:T(8,128)S(1)}, u32[]{:S(2)}, u32[]{:S(2)}) %collective-permute-start.22) | collective-permute-done | bytes 4256 | tf_op jit(solution)/shard_map/ppermute | solution.py:23
  99.6 78.8 %psum.7 = f32[64,64]{0,1:T(8,128)S(1)} all-reduce(f32[64,64]{0,1:T(8,128)S(1)} %fusion.12), channel_id=1, replica_groups=mesh['gx'=32,'gy'=8] {'gx','gy'}, use_global_device_ids=true, to_apply=%region_0.0 | all-reduce | flops 4096 | bytes 32768 | tf_op jit(solution)/shard_map/psum | solution.py:86
  178.5 5.8 %cholesky.17 = f32[64,64]{1,0:T(8,128)S(1)} custom-call(f32[64,64]{1,0:T(8,128)S(1)} %fusion.114), custom_call_target="Cholesky" | custom-call | tf_op jit(solution)/shard_map/jit(cholesky)/cholesky | solution.py:87
  185.7 4.9 %custom-call.7 = f32[1,64,64]{1,2,0:T(8,128)S(1)} custom-call(f32[1,64,64]{2,1,0:T(8,128)S(1)} %fusion.112), custom_call_target="InvertDiagBlocksLowerTriangular" | custom-call | tf_op jit(solution)/shard_map/jit(_solve_triangular)/triangular_solve | solution.py:89
  190.9 1.8 fusion
  192.7 4.4 %copy.72 = f32[64,128,128]{2,1,0:T(8,128)} copy(f32[64,128,128]{2,0,1:T(8,128)S(1)} %fusion) | data formatting | bytes 8388608
  (109 shorter events, 23.3 us)
Async XLA Ops:
  1.4 9.6 %collective-permute-start.1 = (f32[4,2,128]{2,1,0:T(2,128)S(1)}, f32[4,2,128]{2,1,0:T(2,128)S(1)}, u32[]{:S(2)}, u32[]{:S(2)}) collective-permute-start(f32[4,2,128]{2,1,0:T(2,128)S(1)} %get-tuple-element.73), channel_id=1, source_target_pairs={{0,8},{8,16},{16,24},{24,32},{32,40},{40,48},{48,56},{56,64},{64,7... | collective-permute-start | bytes 12296 | tf_op jit(solution)/shard_map/ppermute | solution.py:20
  3.9 7.1 %collective-permute-start = (f32[4,2,128]{2,1,0:T(2,128)S(1)}, f32[4,2,128]{2,1,0:T(2,128)S(1)}, u32[]{:S(2)}, u32[]{:S(2)}) collective-permute-start(f32[4,2,128]{2,1,0:T(2,128)S(1)} %get-tuple-element.74), channel_id=1, source_target_pairs={{8,0},{16,8},{24,16},{32,24},{40,32},{48,40},{56,48},{64,56},{72,6... | collective-permute-start | bytes 12296 | tf_op jit(solution)/shard_map/ppermute | solution.py:23
  12.2 7.3 %collective-permute-start.2 = (f32[4,132,2]{2,1,0:T(8,128)S(1)}, f32[4,132,2]{2,1,0:T(8,128)S(1)}, u32[]{:S(2)}, u32[]{:S(2)}) collective-permute-start(f32[4,132,2]{2,1,0:T(8,128)S(1)} %get-tuple-element.60), channel_id=1, source_target_pairs={{1,0},{2,1},{3,2},{4,3},{5,4},{6,5},{7,6},{0,7},{9,8},{10,9},{11,1... | collective-permute-start | bytes 12680 | tf_op jit(solution)/shard_map/ppermute | solution.py:23
  13.7 5.7 %collective-permute-start.3 = (f32[4,132,2]{2,1,0:T(8,128)S(1)}, f32[4,132,2]{2,1,0:T(8,128)S(1)}, u32[]{:S(2)}, u32[]{:S(2)}) collective-permute-start(f32[4,132,2]{2,1,0:T(8,128)S(1)} %get-tuple-element.61), channel_id=1, source_target_pairs={{0,1},{1,2},{2,3},{3,4},{4,5},{5,6},{6,7},{7,0},{8,9},{9,10},{10,1... | collective-permute-start | bytes 12680 | tf_op jit(solution)/shard_map/ppermute | solution.py:20
  21.7 6.2 %collective-permute-start.5 = (f32[4,2,128]{2,1,0:T(2,128)S(1)}, f32[4,2,128]{2,1,0:T(2,128)S(1)}, u32[]{:S(2)}, u32[]{:S(2)}) collective-permute-start(f32[4,2,128]{2,1,0:T(2,128)S(1)} %get-tuple-element.70), channel_id=1, source_target_pairs={{0,8},{8,16},{16,24},{24,32},{32,40},{40,48},{48,56},{56,64},{64,7... | collective-permute-start | bytes 12296 | tf_op jit(solution)/shard_map/ppermute | solution.py:20
  21.8 6.1 %collective-permute-start.4 = (f32[4,2,128]{2,1,0:T(2,128)S(1)}, f32[4,2,128]{2,1,0:T(2,128)S(1)}, u32[]{:S(2)}, u32[]{:S(2)}) collective-permute-start(f32[4,2,128]{2,1,0:T(2,128)S(1)} %get-tuple-element.71), channel_id=1, source_target_pairs={{8,0},{16,8},{24,16},{32,24},{40,32},{48,40},{56,48},{64,56},{72,6... | collective-permute-start | bytes 12296 | tf_op jit(solution)/shard_map/ppermute | solution.py:23
  28.1 6.6 %collective-permute-start.6 = (f32[4,132,2]{2,1,0:T(8,128)S(1)}, f32[4,132,2]{2,1,0:T(8,128)S(1)}, u32[]{:S(2)}, u32[]{:S(2)}) collective-permute-start(f32[4,132,2]{2,1,0:T(8,128)S(1)} %get-tuple-element.58), channel_id=1, source_target_pairs={{1,0},{2,1},{3,2},{4,3},{5,4},{6,5},{7,6},{0,7},{9,8},{10,9},{11,1... | collective-permute-start | bytes 12680 | tf_op jit(solution)/shard_map/ppermute | solution.py:23
  32.0 3.5 %collective-permute-start.7 = (f32[4,132,2]{2,1,0:T(8,128)S(1)}, f32[4,132,2]{2,1,0:T(8,128)S(1)}, u32[]{:S(2)}, u32[]{:S(2)}) collective-permute-start(f32[4,132,2]{2,1,0:T(8,128)S(1)} %get-tuple-element.59), channel_id=1, source_target_pairs={{0,1},{1,2},{2,3},{3,4},{4,5},{5,6},{6,7},{7,0},{8,9},{9,10},{10,1... | collective-permute-start | bytes 12680 | tf_op jit(solution)/shard_map/ppermute | solution.py:20
  36.2 6.1 %collective-permute-start.9 = (f32[4,2,128]{2,1,0:T(2,128)S(1)}, f32[4,2,128]{2,1,0:T(2,128)S(1)}, u32[]{:S(2)}, u32[]{:S(2)}) collective-permute-start(f32[4,2,128]{2,1,0:T(2,128)S(1)} %get-tuple-element.68), channel_id=1, source_target_pairs={{0,8},{8,16},{16,24},{24,32},{32,40},{40,48},{48,56},{56,64},{64,7... | collective-permute-start | bytes 12296 | tf_op jit(solution)/shard_map/ppermute | solution.py:20
  36.3 6.0 %collective-permute-start.8 = (f32[4,2,128]{2,1,0:T(2,128)S(1)}, f32[4,2,128]{2,1,0:T(2,128)S(1)}, u32[]{:S(2)}, u32[]{:S(2)}) collective-permute-start(f32[4,2,128]{2,1,0:T(2,128)S(1)} %get-tuple-element.69), channel_id=1, source_target_pairs={{8,0},{16,8},{24,16},{32,24},{40,32},{48,40},{56,48},{64,56},{72,6... | collective-permute-start | bytes 12296 | tf_op jit(solution)/shard_map/ppermute | solution.py:23
  42.6 7.6 %collective-permute-start.10 = (f32[4,132,2]{2,1,0:T(8,128)S(1)}, f32[4,132,2]{2,1,0:T(8,128)S(1)}, u32[]{:S(2)}, u32[]{:S(2)}) collective-permute-start(f32[4,132,2]{2,1,0:T(8,128)S(1)} %get-tuple-element.56), channel_id=1, source_target_pairs={{1,0},{2,1},{3,2},{4,3},{5,4},{6,5},{7,6},{0,7},{9,8},{10,9},{11,1... | collective-permute-start | bytes 12680 | tf_op jit(solution)/shard_map/ppermute | solution.py:23
  47.1 3.5 %collective-permute-start.11 = (f32[4,132,2]{2,1,0:T(8,128)S(1)}, f32[4,132,2]{2,1,0:T(8,128)S(1)}, u32[]{:S(2)}, u32[]{:S(2)}) collective-permute-start(f32[4,132,2]{2,1,0:T(8,128)S(1)} %get-tuple-element.57), channel_id=1, source_target_pairs={{0,1},{1,2},{2,3},{3,4},{4,5},{5,6},{6,7},{7,0},{8,9},{9,10},{10,1... | collective-permute-start | bytes 12680 | tf_op jit(solution)/shard_map/ppermute | solution.py:20
  51.5 6.2 %collective-permute-start.13 = (f32[4,2,128]{2,1,0:T(2,128)S(1)}, f32[4,2,128]{2,1,0:T(2,128)S(1)}, u32[]{:S(2)}, u32[]{:S(2)}) collective-permute-start(f32[4,2,128]{2,1,0:T(2,128)S(1)} %get-tuple-element.66), channel_id=1, source_target_pairs={{0,8},{8,16},{16,24},{24,32},{32,40},{40,48},{48,56},{56,64},{64,7... | collective-permute-start | bytes 12296 | tf_op jit(solution)/shard_map/ppermute | solution.py:20
  51.5 6.1 %collective-permute-start.12 = (f32[4,2,128]{2,1,0:T(2,128)S(1)}, f32[4,2,128]{2,1,0:T(2,128)S(1)}, u32[]{:S(2)}, u32[]{:S(2)}) collective-permute-start(f32[4,2,128]{2,1,0:T(2,128)S(1)} %get-tuple-element.67), channel_id=1, source_target_pairs={{8,0},{16,8},{24,16},{32,24},{40,32},{48,40},{56,48},{64,56},{72,6... | collective-permute-start | bytes 12296 | tf_op jit(solution)/shard_map/ppermute | solution.py:23
  57.9 7.6 %collective-permute-start.14 = (f32[4,132,2]{2,1,0:T(8,128)S(1)}, f32[4,132,2]{2,1,0:T(8,128)S(1)}, u32[]{:S(2)}, u32[]{:S(2)}) collective-permute-start(f32[4,132,2]{2,1,0:T(8,128)S(1)} %get-tuple-element.54), channel_id=1, source_target_pairs={{1,0},{2,1},{3,2},{4,3},{5,4},{6,5},{7,6},{0,7},{9,8},{10,9},{11,1... | collective-permute-start | bytes 12680 | tf_op jit(solution)/shard_map/ppermute | solution.py:23
  62.5 3.5 %collective-permute-start.15 = (f32[4,132,2]{2,1,0:T(8,128)S(1)}, f32[4,132,2]{2,1,0:T(8,128)S(1)}, u32[]{:S(2)}, u32[]{:S(2)}) collective-permute-start(f32[4,132,2]{2,1,0:T(8,128)S(1)} %get-tuple-element.55), channel_id=1, source_target_pairs={{0,1},{1,2},{2,3},{3,4},{4,5},{5,6},{6,7},{7,0},{8,9},{9,10},{10,1... | collective-permute-start | bytes 12680 | tf_op jit(solution)/shard_map/ppermute | solution.py:20
  66.7 8.5 %collective-permute-start.17 = (f32[4,2,128]{2,1,0:T(2,128)S(1)}, f32[4,2,128]{2,1,0:T(2,128)S(1)}, u32[]{:S(2)}, u32[]{:S(2)}) collective-permute-start(f32[4,2,128]{2,1,0:T(2,128)S(1)} %get-tuple-element.64), channel_id=1, source_target_pairs={{0,8},{8,16},{16,24},{24,32},{32,40},{40,48},{48,56},{56,64},{64,7... | collective-permute-start | bytes 12296 | tf_op jit(solution)/shard_map/ppermute | solution.py:20
  66.8 8.4 %collective-permute-start.16 = (f32[4,2,128]{2,1,0:T(2,128)S(1)}, f32[4,2,128]{2,1,0:T(2,128)S(1)}, u32[]{:S(2)}, u32[]{:S(2)}) collective-permute-start(f32[4,2,128]{2,1,0:T(2,128)S(1)} %get-tuple-element.65), channel_id=1, source_target_pairs={{8,0},{16,8},{24,16},{32,24},{40,32},{48,40},{56,48},{64,56},{72,6... | collective-permute-start | bytes 12296 | tf_op jit(solution)/shard_map/ppermute | solution.py:23
  75.4 7.0 %collective-permute-start.18 = (f32[4,132,2]{2,1,0:T(8,128)S(1)}, f32[4,132,2]{2,1,0:T(8,128)S(1)}, u32[]{:S(2)}, u32[]{:S(2)}) collective-permute-start(f32[4,132,2]{2,1,0:T(8,128)S(1)} %get-tuple-element.52), channel_id=1, source_target_pairs={{1,0},{2,1},{3,2},{4,3},{5,4},{6,5},{7,6},{0,7},{9,8},{10,9},{11,1... | collective-permute-start | bytes 12680 | tf_op jit(solution)/shard_map/ppermute | solution.py:23
  79.4 3.5 %collective-permute-start.19 = (f32[4,132,2]{2,1,0:T(8,128)S(1)}, f32[4,132,2]{2,1,0:T(8,128)S(1)}, u32[]{:S(2)}, u32[]{:S(2)}) collective-permute-start(f32[4,132,2]{2,1,0:T(8,128)S(1)} %get-tuple-element.53), channel_id=1, source_target_pairs={{0,1},{1,2},{2,3},{3,4},{4,5},{5,6},{6,7},{7,0},{8,9},{9,10},{10,1... | collective-permute-start | bytes 12680 | tf_op jit(solution)/shard_map/ppermute | solution.py:20
  83.6 5.9 %collective-permute-start.21 = (f32[4,2,128]{2,1,0:T(2,128)S(1)}, f32[4,2,128]{2,1,0:T(2,128)S(1)}, u32[]{:S(2)}, u32[]{:S(2)}) collective-permute-start(f32[4,2,128]{2,1,0:T(2,128)S(1)} %get-tuple-element.62), channel_id=1, source_target_pairs={{0,8},{8,16},{16,24},{24,32},{32,40},{40,48},{48,56},{56,64},{64,7... | collective-permute-start | bytes 12296 | tf_op jit(solution)/shard_map/ppermute | solution.py:20
  83.7 5.8 %collective-permute-start.20 = (f32[4,2,128]{2,1,0:T(2,128)S(1)}, f32[4,2,128]{2,1,0:T(2,128)S(1)}, u32[]{:S(2)}, u32[]{:S(2)}) collective-permute-start(f32[4,2,128]{2,1,0:T(2,128)S(1)} %get-tuple-element.63), channel_id=1, source_target_pairs={{8,0},{16,8},{24,16},{32,24},{40,32},{48,40},{56,48},{64,56},{72,6... | collective-permute-start | bytes 12296 | tf_op jit(solution)/shard_map/ppermute | solution.py:23
  89.7 7.9 %collective-permute-start.22 = (f32[4,132,2]{2,1,0:T(8,128)S(1)}, f32[4,132,2]{2,1,0:T(8,128)S(1)}, u32[]{:S(2)}, u32[]{:S(2)}) collective-permute-start(f32[4,132,2]{2,1,0:T(8,128)S(1)} %get-tuple-element.50), channel_id=1, source_target_pairs={{1,0},{2,1},{3,2},{4,3},{5,4},{6,5},{7,6},{0,7},{9,8},{10,9},{11,1... | collective-permute-start | bytes 12680 | tf_op jit(solution)/shard_map/ppermute | solution.py:23
  94.5 3.5 %collective-permute-start.23 = (f32[4,132,2]{2,1,0:T(8,128)S(1)}, f32[4,132,2]{2,1,0:T(8,128)S(1)}, u32[]{:S(2)}, u32[]{:S(2)}) collective-permute-start(f32[4,132,2]{2,1,0:T(8,128)S(1)} %get-tuple-element.51), channel_id=1, source_target_pairs={{0,1},{1,2},{2,3},{3,4},{4,5},{5,6},{6,7},{7,0},{8,9},{9,10},{10,1... | collective-permute-start | bytes 12680 | tf_op jit(solution)/shard_map/ppermute | solution.py:20
  (4 other events, 39.1 us)
where the time goes:
time: 197 us
  blocking collectives  78.8 us (40%)
  starting transfers between devices  59.6 us (30%)
  waiting for transfers between devices  25.9 us (13%)
  other arithmetic  19.7 us (10%)
  local copies, waits for them, and re-layouts  9.39 us (5%)
  matrix products  2.72 us (1%)
    psum x1, blocking collectives, body(): gram = lax.psum(local_gram, ('gx', 'gy'))  78.8 us
    ppermute x12, starting transfers between devices, padded_2(): lax.ppermute(lax.slice_in_dim(block, 0, width, axis=dim), axis, backward)  55.4 us
    ppermute x12, waiting for transfers between devices, padded_2(): lax.ppermute(lax.slice_in_dim(block, 0, width, axis=dim), axis, backward)  18.6 us
    unnamed x14, local copies, waits for them, and re-layouts  7.46 us
    ppermute x12, waiting for transfers between devices, padded_2(): lax.ppermute(lax.slice_in_dim(block, block.shape[dim] - width, None, axis...  7.3 us
    another operation x3, other arithmetic, body(): lower_factor = jnp.linalg.cholesky(gram)  6.52 us
    another operation x2, other arithmetic, body(): jax.scipy.linalg.solve_triangular(lower_factor, identity_matrix, lower=True)  5.55 us
    div x6, other arithmetic, derivative_y(): return (8.0 * (ahead_one - behind_one) - (ahead_two - behind_two)) / 12.0  4.75 us
  transfers between devices with their start and end apart: 24, of which 16 were waited for; matrix products, arithmetic and copies ran while one was open for 2% of the time, Pallas kernels for 0%

commit v1 on v0

v1 whole, which is shorter than its diff:
```python
import functools

import jax
import jax.numpy as jnp
from jax import lax
from jax.experimental import pallas as pl
from jax.experimental.pallas import tpu as pltpu
from jax.sharding import PartitionSpec as P

MESH = pl.DeviceIdType.MESH
STEPS = 2
courant = 0.8
stream_speed = 0.3
span_speed = 0.1

MODES = 64
RESIDENT = 62
TILE = 128
HALO = 12
PAD = 16
ROWS = TILE + 2 * PAD
FIELDS = 5
GX = 32
GY = 8


def lanes(shape):
    return lax.broadcasted_iota(jnp.int32, shape, len(shape) - 1)


def slope_x(ref, field, row, rows):
    near = ref[field, pl.ds(row + 1, rows), :] - ref[field, pl.ds(row - 1, rows), :]
    far = ref[field, pl.ds(row + 2, rows), :] - ref[field, pl.ds(row - 2, rows), :]
    return (2.0 / 3.0) * near - (1.0 / 12.0) * far


def slope_y(main, edge, first, last):
    def pair(amount):
        a, b = pltpu.roll(main, amount, 1), pltpu.roll(edge, amount, 1)
        wrapped = last[amount] if amount > 64 else first[amount]
        return jnp.where(wrapped, b, a), jnp.where(wrapped, a, b)

    ahead_one, behind_one = pair(TILE - 1), pair(1)
    ahead_two, behind_two = pair(TILE - 2), pair(2)
    return tuple(
        (2.0 / 3.0) * (a1 - b1) - (1.0 / 12.0) * (a2 - b2)
        for a1, b1, a2, b2 in zip(ahead_one, behind_one, ahead_two, behind_two)
    )


def stage(kind, state, source, target, sound):
    rows = 8
    lane = lanes((rows, TILE))
    first = {1: lane < 1, 2: lane < 2}
    last = {TILE - 1: lane >= TILE - 1, TILE - 2: lane >= TILE - 2}

    def chunk(index, carry):
        row = pl.multiple_of(8 + index * rows, rows)
        here = pl.ds(row, rows)
        centre = [[source[s][f, here, :] for f in range(4)] for s in range(2)]
        dx = [[slope_x(source[s], f, row, rows) for f in range(4)] for s in range(2)]
        both = [slope_y(centre[0][f], centre[1][f], first, last) for f in range(4)]
        for s in range(2):
            dy = [both[f][s] for f in range(4)]
            diverge = dx[s][1] + dy[2]
            advect = [stream_speed * dx[s][f] + span_speed * dy[f] for f in range(4)]
            rate = [
                advect[0] + diverge,
                advect[1] + dx[s][3],
                advect[2] + dy[3],
                advect[3] + sound[s][4, here, :] * diverge,
            ]
            for f in range(4):
                moved = centre[s][f] - courant * rate[f]
                if kind == 2:
                    moved = 0.75 * state[s][f, here, :] + 0.25 * moved
                elif kind == 3:
                    moved = (1.0 / 3.0) * state[s][f, here, :] + (2.0 / 3.0) * moved
                target[s][f, here, :] = moved
        return carry

    lax.fori_loop(0, (ROWS - 16) // rows, chunk, 0)


def wide_kernel(
    flow_hbm, sound_hbm, snap_hbm, state_out, block_out, gram_out,
    snap, block, tile, edge, first_main, first_edge, second_main, second_edge,
    strip, left_strip, right_strip, packed, part_one, part_two, total_two, whole,
    load_sem, halo_send, halo_recv, sum_send, sum_recv,
):
    gx, gy = lax.axis_index("gx"), lax.axis_index("gy")
    core = lax.rem(gy, 2)

    def at(dx, dy):
        return (lax.rem(gx + (dx + GX), GX), lax.rem(gy + (dy + GY), GY))

    row_peers = [at(d, 0) for d in range(1, GX)]
    column_peers = [at(0, d) for d in range(1, GY)]
    corner_peers = [at(dx, dy) for dx in (-1, 1) for dy in (-1, 1)]
    everyone = row_peers + column_peers + corner_peers

    barrier = pltpu.get_barrier_semaphore()
    for peer in everyone:
        pl.semaphore_signal(barrier, inc=1, device_id=peer, device_id_type=MESH)

    inside = pl.ds(PAD, TILE)
    loads = [
        pltpu.make_async_copy(flow_hbm, tile.at[pl.ds(0, 4), inside, :], load_sem.at[0]),
        pltpu.make_async_copy(sound_hbm, tile.at[4, inside, :], load_sem.at[1]),
        pltpu.make_async_copy(snap_hbm, snap.at[pl.ds(0, RESIDENT)], load_sem.at[2]),
    ]
    for load in loads:
        load.start()
    loads[0].wait()
    loads[1].wait()

    def pack(index, carry):
        row = pl.multiple_of(index * 16, 16)
        lane = lanes((16, TILE))
        gathered = pltpu.roll(tile[0, pl.ds(PAD + row, 16), :], HALO, 1)
        for f in range(1, FIELDS):
            moved = pltpu.roll(tile[f, pl.ds(PAD + row, 16), :], HALO + 24 * f, 1)
            gathered = jnp.where(lane >= 24 * f, moved, gathered)
        strip[pl.ds(row, 16), :] = gathered
        return carry

    lax.fori_loop(0, TILE // 16, pack, 0)
    pl.semaphore_wait(barrier, len(everyone))

    top, bottom = pl.ds(0, PAD), pl.ds(PAD + TILE, PAD)
    low, high = pl.ds(0, PAD), pl.ds(TILE - PAD, PAD)
    moves = [
        (tile.at[:, pl.ds(TILE, PAD), :], tile.at[:, top, :], at(1, 0)),
        (tile.at[:, pl.ds(PAD, PAD), :], tile.at[:, bottom, :], at(-1, 0)),
        (strip, left_strip.at[inside, :], at(0, 1)),
        (strip, right_strip.at[inside, :], at(0, -1)),
        (strip.at[high, :], left_strip.at[top, :], at(1, 1)),
        (strip.at[low, :], left_strip.at[bottom, :], at(-1, 1)),
        (strip.at[high, :], right_strip.at[top, :], at(1, -1)),
        (strip.at[low, :], right_strip.at[bottom, :], at(-1, -1)),
    ]
    halos = []
    for number, (source, target, peer) in enumerate(moves):
        halos.append(
            pltpu.make_async_remote_copy(
                src_ref=source, dst_ref=target, send_sem=halo_send.at[number],
                recv_sem=halo_recv.at[number], device_id=peer, device_id_type=MESH,
            )
        )
        halos[-1].start()

    loads[2].wait()

    for group in range(3):
        modes = pl.ds(group * 16, 16)
        for row in range(0, TILE, 16):
            turned = jnp.swapaxes(snap[modes, row : row + 16, :], 0, 1)
            for i in range(16):
                block[modes, (row + i) * TILE : (row + i + 1) * TILE] = turned[i]

    for halo in halos:
        halo.wait()

    def unpack(index, carry):
        here = pl.ds(pl.multiple_of(index * 16, 16), 16)
        lane = lanes((16, TILE))
        merged = jnp.where(lax.rem(lane, 24) >= HALO, right_strip[here, :], left_strip[here, :])
        for f in range(FIELDS):
            edge[f, here, :] = pltpu.roll(merged, TILE - (24 * f + HALO), 1)
        return carry

    lax.fori_loop(0, ROWS // 16, unpack, 0)

    state = (tile, edge)
    one, two = (first_main, first_edge), (second_main, second_edge)
    pressures = []
    for step in range(STEPS):
        stage(1, state, state, one, state)
        stage(2, state, one, two, state)
        stage(3, state, two, state, state)
        snap[RESIDENT + step] = tile[3, inside, :].astype(jnp.bfloat16)

    state_out[...] = tile[0:4, inside, :]

    last = pl.ds(48, 16)
    for row in range(0, TILE, 16):
        turned = jnp.swapaxes(snap[last, row : row + 16, :], 0, 1)
        for i in range(16):
            block[last, (row + i) * TILE : (row + i + 1) * TILE] = turned[i]

    save = pltpu.make_async_copy(block, block_out, load_sem.at[2])
    save.start()
    gram = lax.dot_general(
        block[...], block[...], (((1,), (1,)), ((), ())), preferred_element_type=jnp.float32
    ) * (1.0 / (GX * GY * TILE * TILE))
    folded = jnp.concatenate([gram[32:64], gram[0:32]], axis=1)
    packed[0] = folded[0:16]
    packed[1] = folded[16:32]

    for number, peer in enumerate(column_peers):
        pltpu.make_async_remote_copy(
            src_ref=packed.at[lax.rem(peer[1], 2)], dst_ref=part_one.at[number],
            send_sem=sum_send.at[0], recv_sem=sum_recv.at[0], device_id=peer, device_id_type=MESH,
        ).start()
    pltpu.make_async_copy(part_one, part_one, sum_recv.at[0]).wait()
    total = packed[core]
    for number in range(GY - 1):
        total = total + part_one[number]
    total_two[...] = total
    pltpu.make_async_copy(part_one, part_one, sum_send.at[0]).wait()

    for number, peer in enumerate(row_peers):
        pltpu.make_async_remote_copy(
            src_ref=total_two, dst_ref=part_two.at[number],
            send_sem=sum_send.at[1], recv_sem=sum_recv.at[1], device_id=peer, device_id_type=MESH,
        ).start()
    pltpu.make_async_copy(part_two, part_two, sum_recv.at[1]).wait()

    def add(number, so_far):
        return so_far + part_two[number]

    total = lax.fori_loop(0, GX - 1, add, total_two[...])
    pltpu.make_async_copy(part_two, part_two, sum_send.at[1]).wait()
    whole[core] = total

    partner = (gx, gy + 1 - 2 * core)
    swap = pltpu.make_async_remote_copy(
        src_ref=whole.at[core], dst_ref=whole.at[core],
        send_sem=sum_send.at[2], recv_sem=sum_recv.at[2], device_id=partner, device_id_type=MESH,
    )
    swap.start()
    swap.wait()
    gram_out[...] = whole[...]
    save.wait()


def basis_kernel(gram_ref, block_ref, state_hbm, basis_ref, state_out, weight, sem):
    step = pl.program_id(0)
    move = pltpu.make_async_copy(state_hbm, state_out, sem)

    @pl.when(step == 0)
    def _():
        move.start()
        folded = jnp.concatenate([gram_ref[0], gram_ref[1]], axis=0)
        gram = jnp.concatenate([pltpu.roll(folded, 64, 1), folded], axis=0)
        row = lax.broadcasted_iota(jnp.int32, (MODES, TILE), 0)
        lane = lanes((MODES, TILE))
        work = jnp.where(lane < MODES, gram, jnp.where(lane == row + MODES, 1.0, 0.0))
        for k in range(MODES):
            start = (k // 8) * 8
            column = jnp.broadcast_to(work[start:, k : k + 1], (MODES - start, TILE))
            pivot_row = work[k : k + 1, :]
            scaled = pivot_row / column[k - start : k - start + 1, :]
            below = row[start:] > k
            changed = work[start:] - jnp.where(below, column * scaled, 0.0)
            work = jnp.concatenate([work[:start], changed], axis=0) if start else changed
        diagonal = jnp.sum(jnp.where(lane == row, work, 0.0), axis=1, keepdims=True)
        inverse = work[:, MODES:] * (1.0 / jnp.sqrt(diagonal))
        high = inverse.astype(jnp.bfloat16)
        rest = inverse - high.astype(jnp.float32)
        middle = rest.astype(jnp.bfloat16)
        low = (rest - middle.astype(jnp.float32)).astype(jnp.bfloat16)
        weight[...] = jnp.concatenate([high, middle, low], axis=1)

    for start in range(0, basis_ref.shape[1], 8):
        part = block_ref[:, start * TILE : (start + 8) * TILE]
        rows = jnp.dot(
            weight[...], jnp.concatenate([part, part, part], axis=0), preferred_element_type=jnp.float32
        )
        stacked = jnp.stack([rows[:, i * TILE : (i + 1) * TILE] for i in range(8)], axis=0)
        basis_ref[:, start : start + 8, :] = jnp.swapaxes(stacked, 0, 1)

    @pl.when(step == pl.num_programs(0) - 1)
    def _():
        move.wait()


def body(flow_state, sound_speed_sq, snapshots):
    anywhere = pl.BlockSpec(memory_space=pl.ANY)
    local = pl.BlockSpec(memory_space=pltpu.VMEM)
    field = (FIELDS, ROWS, TILE)
    f32, bf16 = jnp.float32, jnp.bfloat16
    new_state, block, gram = pl.pallas_call(
        wide_kernel,
        out_shape=(
            jax.ShapeDtypeStruct((4, TILE, TILE), f32),
            jax.ShapeDtypeStruct((MODES, TILE * TILE), bf16),
            jax.ShapeDtypeStruct((2, 16, TILE), f32),
        ),
        in_specs=[anywhere] * 3,
        out_specs=(local, anywhere, local),
        scratch_shapes=[
            pltpu.VMEM((MODES, TILE, TILE), bf16),
            pltpu.VMEM((MODES, TILE * TILE), bf16),
            pltpu.VMEM(field, f32),
            pltpu.VMEM(field, f32),
            pltpu.VMEM((4, ROWS, TILE), f32),
            pltpu.VMEM((4, ROWS, TILE), f32),
            pltpu.VMEM((4, ROWS, TILE), f32),
            pltpu.VMEM((4, ROWS, TILE), f32),
            pltpu.VMEM((TILE, TILE), f32),
            pltpu.VMEM((ROWS, TILE), f32),
            pltpu.VMEM((ROWS, TILE), f32),
            pltpu.VMEM((2, 16, TILE), f32),
            pltpu.VMEM((GY - 1, 16, TILE), f32),
            pltpu.VMEM((GX - 1, 16, TILE), f32),
            pltpu.VMEM((16, TILE), f32),
            pltpu.VMEM((2, 16, TILE), f32),
            pltpu.SemaphoreType.DMA((3,)),
            pltpu.SemaphoreType.DMA((8,)),
            pltpu.SemaphoreType.DMA((8,)),
            pltpu.SemaphoreType.DMA((3,)),
            pltpu.SemaphoreType.DMA((3,)),
        ],
        compiler_params=pltpu.CompilerParams(
            collective_id=0, has_side_effects=True, vmem_limit_bytes=40 << 20
        ),
        name="flow_and_gram",
    )(flow_state, sound_speed_sq, snapshots)

    rows = 32
    pod_basis, new_state = pl.pallas_call(
        basis_kernel,
        grid=(TILE // rows,),
        out_shape=(
            jax.ShapeDtypeStruct((MODES, TILE, TILE), f32),
            jax.ShapeDtypeStruct((4, TILE, TILE), f32),
        ),
        in_specs=[
            pl.BlockSpec((2, 16, TILE), lambda i: (0, 0, 0)),
            pl.BlockSpec((MODES, rows * TILE), lambda i: (0, i)),
            anywhere,
        ],
        out_specs=(pl.BlockSpec((MODES, rows, TILE), lambda i: (0, i, 0)), anywhere),
        scratch_shapes=[pltpu.VMEM((MODES, 3 * MODES), bf16), pltpu.SemaphoreType.DMA],
        compiler_params=pltpu.CompilerParams(vmem_limit_bytes=20 << 20),
        name="basis",
    )(gram, block, new_state)
    return new_state, pod_basis


def solution(mesh):
    placed = (P(None, "gx", "gy"), P("gx", "gy"), P(None, "gx", "gy"))
    return jax.shard_map(
        body,
        mesh=mesh,
        in_specs=placed,
        out_specs=(P(None, "gx", "gy"), P(None, "gx", "gy")),
        check_vma=False,
    )
```

time: 197 us -> 57.2 us (0.29)
  blocking collectives: 78.8 us -> 0 us
  starting transfers between devices: 59.6 us -> 0 us
  Pallas kernels: 0 us -> 53 us
  waiting for transfers between devices: 25.9 us -> 0 us
  other arithmetic: 19.7 us -> 0 us
  local copies, waits for them, and re-layouts: 9.39 us -> 3.35 us
  matrix products: 2.72 us -> 0 us
    psum x1 -> x0, blocking collectives: 78.8 us -> none  [body(): gram = lax.psum(local_gram, ('gx', 'gy'))]
    ppermute x24 -> x0, starting transfers between devices: 59.6 us -> none  [the longest x12 55.4 us: padded_2(): lax.ppermute(lax.slice_in_dim(block, 0, width, axis=dim), axis, backward)]
    pallas_call x0 -> x2, Pallas kernels: none -> 53 us  [the longest x1 44 us: body(): pl.pallas_call(wide_kernel, out_shape=(jax.ShapeDtypeStruct((4, TILE, TIL...]
    ppermute x24 -> x0, waiting for transfers between devices: 25.9 us -> none  [the longest x12 18.6 us: padded_2(): lax.ppermute(lax.slice_in_dim(block, 0, width, axis=dim), axis, backward)]
    another operation x11 -> x0, other arithmetic: 12.2 us -> none  [the longest x3 6.52 us: body(): lower_factor = jnp.linalg.cholesky(gram)]
    div x13 -> x0, other arithmetic: 5.49 us -> none  [the longest x6 4.75 us: derivative_y(): return (8.0 * (ahead_one - behind_one) - (ahead_two - behind_two)) / 12.0]
    unnamed x14 -> x6, local copies, waits for them, and re-layouts: 7.46 us -> 3.35 us
    dot_general x2 -> x0, matrix products: 2.49 us -> none  [the longest x1 1.79 us: body(): jnp.dot(inverse, flat_block.astype(jnp.float32), precision=lax.Precision....]
  transfers between devices with their start and end apart: 24 -> 0, of which waited for: 16 -> 0; matrix products, arithmetic and copies ran while one was open for 2% -> 0% of each run, Pallas kernels for 0% -> 0%
where the time goes in v1:
time: 57.2 us; the launch traced here: 57 us
  Pallas kernels  53 us (93%)
  local copies, waits for them, and re-layouts  3.35 us (6%)
  between operations  0.65 us (1%)
    pallas_call x1, Pallas kernels, body(): pl.pallas_call(wide_kernel, out_shape=(jax.ShapeDtypeStruct((4, TILE, TIL...  44 us
    pallas_call x1, Pallas kernels, body(): pl.pallas_call(basis_kernel, grid=(TILE // rows,), out_shape=(jax.ShapeDt...  8.98 us
    unnamed x6, local copies, waits for them, and re-layouts  3.35 us

profile of v1, /device:TPU:1, one launch (start us, length us, event | category | flops | bytes accessed | tf_op | source)
XLA Modules:
  0.0 57.0 jit_solution(7229924412156691224)
XLA Ops:
  0.6 0.0 copy-start
  0.6 1.6 %copy-done = bf16[62,128,128]{2,1,0:T(8,128)(2,1)S(1)} copy-done((bf16[62,128,128]{2,1,0:T(8,128)(2,1)S(1)}, bf16[62,128,128]{2,1,0:T(8,128)(2,1)}, u32[]{:S(2)}) %copy-start) | copy-done | bytes 2031640
  2.2 0.0 copy-start.1
  2.2 0.9 %copy-done.1 = f32[4,128,128]{2,1,0:T(8,128)S(1)} copy-done((f32[4,128,128]{2,1,0:T(8,128)S(1)}, f32[4,128,128]{2,1,0:T(8,128)}, u32[]{:S(2)}) %copy-start.1) | copy-done | bytes 262168
  3.1 0.0 copy-start.2
  3.2 0.8 %copy-done.2 = f32[128,128]{1,0:T(8,128)S(1)} copy-done((f32[128,128]{1,0:T(8,128)S(1)}, f32[128,128]{1,0:T(8,128)}, u32[]{:S(2)}) %copy-start.2) | copy-done | bytes 65560
  4.0 44.0 %flow_and_gram.1 = (f32[4,128,128]{2,1,0:T(8,128)S(1)}, bf16[64,16384]{1,0:T(8,128)(2,1)S(1)}, f32[2,16,128]{2,1,0:T(8,128)S(1)}) custom-call(f32[4,128,128]{2,1,0:T(8,128)S(1)} %copy-done.1, f32[128,128]{1,0:T(8,128)S(1)} %copy-done.2, bf16[62,128,128]{2,1,0:T(8,128)(2,1)S(1)} %copy-done), custom_call_target="tpu_custom_call" | custom-call | tf_op jit(solution)/shard_map/flow_and_gram/pallas_call | solution.py:283
  48.0 9.0 %basis.1 = (f32[64,128,128]{2,1,0:T(8,128)}, f32[4,128,128]{2,1,0:T(8,128)}) custom-call(f32[2,16,128]{2,1,0:T(8,128)S(1)} %get-tuple-element.7.gram_ref, bf16[64,16384]{1,0:T(8,128)(2,1)S(1)} %get-tuple-element.8.block_ref, f32[4,128,128]{2,1,0:T(8,128)S(1)} %get-tuple-element.9.state_hbm), custom_call_target="tpu_custom_call" | custom-call | tf_op jit(solution)/shard_map/basis/pallas_call | solution.py:322
Async XLA Ops:
  0.6 1.6 %copy-start = (bf16[62,128,128]{2,1,0:T(8,128)(2,1)S(1)}, bf16[62,128,128]{2,1,0:T(8,128)(2,1)}, u32[]{:S(2)}) copy-start(bf16[62,128,128]{2,1,0:T(8,128)(2,1)} %snap_hbm.1) | copy-start | bytes 6094852
  2.2 0.9 %copy-start.1 = (f32[4,128,128]{2,1,0:T(8,128)S(1)}, f32[4,128,128]{2,1,0:T(8,128)}, u32[]{:S(2)}) copy-start(f32[4,128,128]{2,1,0:T(8,128)} %flow_hbm.1) | copy-start | bytes 786436
  3.1 0.8 %copy-start.2 = (f32[128,128]{1,0:T(8,128)S(1)}, f32[128,128]{1,0:T(8,128)}, u32[]{:S(2)}) copy-start(f32[128,128]{1,0:T(8,128)} %sound_hbm.1) | copy-start | bytes 196612

commit v2 on v1

v2 whole, which is shorter than its diff:
```python
import jax
import jax.numpy as jnp
from jax import lax
from jax.experimental import pallas as pl
from jax.experimental.pallas import tpu as pltpu
from jax.sharding import PartitionSpec as P

MESH = pl.DeviceIdType.MESH
STEPS = 2
courant = 0.8
stream_speed = 0.3
span_speed = 0.1

MODES = 64
RESIDENT = 62
TILE = 128
HALO = 12
PAD = 16
ROWS = TILE + 2 * PAD
FIELDS = 5
GX = 32
GY = 8


def lanes(shape):
    return lax.broadcasted_iota(jnp.int32, shape, len(shape) - 1)


def slope_rows(ref, window, field, row, rows):
    near = ref[window, field, pl.ds(row + 1, rows), :] - ref[window, field, pl.ds(row - 1, rows), :]
    far = ref[window, field, pl.ds(row + 2, rows), :] - ref[window, field, pl.ds(row - 2, rows), :]
    return 8.0 * near - far


def slope_lanes(value):
    near = pltpu.roll(value, TILE - 1, 1) - pltpu.roll(value, 1, 1)
    far = pltpu.roll(value, TILE - 2, 1) - pltpu.roll(value, 2, 1)
    return 8.0 * near - far


def stage(kind, margin, state, source, target, sound):
    rows, scale = 8, courant / 12.0
    for row in range(PAD - margin, PAD + TILE + margin, rows):
        here = pl.ds(row, rows)
        for w in range(2):
            centre = [source[w, f, here, :] for f in range(4)]
            dx = [slope_rows(source, w, f, row, rows) for f in range(4)]
            dy = [slope_lanes(centre[f]) for f in range(4)]
            diverge = dx[1] + dy[2]
            advect = [stream_speed * dx[f] + span_speed * dy[f] for f in range(4)]
            rate = [
                advect[0] + diverge,
                advect[1] + dx[3],
                advect[2] + dy[3],
                advect[3] + sound[w, 4, here, :] * diverge,
            ]
            for f in range(4):
                if kind == 1:
                    moved = centre[f] - scale * rate[f]
                elif kind == 2:
                    moved = 0.75 * state[w, f, here, :] + (0.25 * centre[f] - (0.25 * scale) * rate[f])
                else:
                    moved = (1.0 / 3.0) * state[w, f, here, :] + (
                        (2.0 / 3.0) * centre[f] - (2.0 / 3.0 * scale) * rate[f]
                    )
                target[w, f, here, :] = moved


def joined(wide, field, row, rows):
    here = pl.ds(PAD + row, rows)
    lane = lanes((rows, TILE))
    first = (lane >= HALO) & (lane < 64)
    both = jnp.where(first, wide[0, field, here, :], wide[1, field, here, :])
    return pltpu.roll(both, TILE - HALO, 1)


def spread(row):
    return jnp.broadcast_to(row, (8, TILE))


def inverse_factor(gram):
    count = MODES // 8
    lane, sub = lanes((8, TILE)), lax.broadcasted_iota(jnp.int32, (8, TILE), 0)
    tiles = [
        jnp.where(lane < MODES, gram[8 * r : 8 * r + 8], jnp.where(lane == MODES + 8 * r + sub, 1.0, 0.0))
        for r in range(count)
    ]
    for t in range(count):
        column = {
            (j, r): jnp.broadcast_to(tiles[r][:, 8 * t + j : 8 * t + j + 1], (8, TILE))
            for j in range(8)
            for r in range(t, count)
        }
        for j in range(8):
            inverse_pivot = 1.0 / spread(column[j, t][j : j + 1, :])
            factor = {r: column[j, r] * inverse_pivot for r in range(t, count)}
            factor[t] = jnp.where(sub > j, factor[t], 0.0)
            for later in range(j + 1, 8):
                entry = spread(column[later, t][j : j + 1, :])
                for r in range(t, count):
                    column[later, r] = column[later, r] - factor[r] * entry
            pivot_row = spread(tiles[t][j : j + 1, :])
            for r in range(t, count):
                tiles[r] = tiles[r] - factor[r] * pivot_row
    rows = []
    for r in range(count):
        diagonal = jnp.sum(jnp.where(lane == 8 * r + sub, tiles[r], 0.0), axis=1, keepdims=True)
        scaled = pltpu.roll(tiles[r] * (1.0 / jnp.sqrt(diagonal)), MODES, 1)
        rows.append(jnp.where(lane < MODES, scaled, 0.0))
    return jnp.concatenate(rows, axis=0)


def exact_dot(a, b, contract):
    return lax.dot_general(
        a, b, (contract, ((), ())), precision=lax.Precision.HIGHEST, preferred_element_type=jnp.float32
    )


def turn(snap, block, group):
    modes = pl.ds(group * 16, 16)
    for row in range(0, TILE, 16):
        turned = jnp.swapaxes(snap[modes, row : row + 16, :], 0, 1)
        for i in range(16):
            block[modes, (row + i) * TILE : (row + i + 1) * TILE] = turned[i]


def wide_kernel(
    flow_hbm, sound_hbm, snap_hbm, state_out, block, inverse_out,
    snap, tile, wide, one, two, strip, left_strip, right_strip,
    packed, part_one, part_two, total_two, whole,
    late, late_one, late_two, late_total,
    load_sem, halo_send, halo_recv, sum_send, sum_recv,
):
    gx, gy = lax.axis_index("gx"), lax.axis_index("gy")
    core = lax.rem(gy, 2)
    cells = GX * GY * TILE * TILE

    def at(dx, dy):
        return (lax.rem(gx + (dx + GX), GX), lax.rem(gy + (dy + GY), GY))

    row_peers = [at(d, 0) for d in range(1, GX)]
    column_peers = [at(0, d) for d in range(1, GY)]
    corner_peers = [at(dx, dy) for dx in (-1, 1) for dy in (-1, 1)]
    everyone = row_peers + column_peers + corner_peers

    barrier = pltpu.get_barrier_semaphore()
    for peer in everyone:
        pl.semaphore_signal(barrier, inc=1, device_id=peer, device_id_type=MESH)

    inside = pl.ds(PAD, TILE)
    loads = [
        pltpu.make_async_copy(flow_hbm, tile.at[pl.ds(0, 4), inside, :], load_sem.at[0]),
        pltpu.make_async_copy(sound_hbm, tile.at[4, inside, :], load_sem.at[1]),
        pltpu.make_async_copy(snap_hbm, snap.at[pl.ds(0, RESIDENT)], load_sem.at[2]),
    ]
    for load in loads:
        load.start()
    snap[RESIDENT:MODES] = jnp.zeros((MODES - RESIDENT, TILE, TILE), jnp.bfloat16)
    loads[0].wait()
    loads[1].wait()

    lane = lanes((16, TILE))
    for row in range(0, TILE, 16):
        gathered = pltpu.roll(tile[0, pl.ds(PAD + row, 16), :], HALO, 1)
        for f in range(1, FIELDS):
            moved = pltpu.roll(tile[f, pl.ds(PAD + row, 16), :], HALO + 24 * f, 1)
            gathered = jnp.where(lane >= 24 * f, moved, gathered)
        strip[pl.ds(row, 16), :] = gathered

    loads[2].wait()
    for group in range(4):
        turn(snap, block, group)
    gram = lax.dot_general(
        block[...], block[...], (((1,), (1,)), ((), ())), preferred_element_type=jnp.float32
    ) * (1.0 / cells)
    folded = jnp.concatenate([gram[32:64], gram[0:32]], axis=1)
    packed[0] = folded[0:16]
    packed[1] = folded[16:32]

    pl.semaphore_wait(barrier, len(everyone))

    top, bottom = pl.ds(0, PAD), pl.ds(PAD + TILE, PAD)
    low, high = pl.ds(0, PAD), pl.ds(TILE - PAD, PAD)
    moves = [
        (tile.at[:, pl.ds(TILE, PAD), :], tile.at[:, top, :], at(1, 0)),
        (tile.at[:, pl.ds(PAD, PAD), :], tile.at[:, bottom, :], at(-1, 0)),
        (strip, left_strip.at[inside, :], at(0, 1)),
        (strip, right_strip.at[inside, :], at(0, -1)),
        (strip.at[high, :], left_strip.at[top, :], at(1, 1)),
        (strip.at[low, :], left_strip.at[bottom, :], at(-1, 1)),
        (strip.at[high, :], right_strip.at[top, :], at(1, -1)),
        (strip.at[low, :], right_strip.at[bottom, :], at(-1, -1)),
    ]
    halos = []
    for number, (source, target, peer) in enumerate(moves):
        halos.append(
            pltpu.make_async_remote_copy(
                src_ref=source, dst_ref=target, send_sem=halo_send.at[number],
                recv_sem=halo_recv.at[number], device_id=peer, device_id_type=MESH,
            )
        )
        halos[-1].start()

    def send(source, target, slot, peer):
        copy = pltpu.make_async_remote_copy(
            src_ref=source, dst_ref=target, send_sem=sum_send.at[slot],
            recv_sem=sum_recv.at[slot], device_id=peer, device_id_type=MESH,
        )
        copy.start()
        return copy

    def received(ref, slot):
        pltpu.make_async_copy(ref, ref, sum_recv.at[slot]).wait()

    def sent(ref, slot):
        pltpu.make_async_copy(ref, ref, sum_send.at[slot]).wait()

    for number, peer in enumerate(column_peers):
        send(packed.at[lax.rem(peer[1], 2)], part_one.at[number], 0, peer)

    for halo in halos:
        halo.wait()
    for row in range(0, ROWS, 16):
        here = pl.ds(row, 16)
        merged = jnp.where(lax.rem(lane, 24) >= HALO, right_strip[here, :], left_strip[here, :])
        for f in range(FIELDS):
            beside = pltpu.roll(merged, TILE - 24 * f, 1) if f else merged
            turned = pltpu.roll(tile[f, here, :], HALO, 1)
            wide[0, f, here, :] = jnp.where(lane < HALO, beside, turned)
            wide[1, f, here, :] = jnp.where((lane >= HALO) & (lane < 2 * HALO), beside, turned)

    stage(1, 10, wide, wide, one, wide)

    received(part_one, 0)
    total = packed[core]
    for number in range(GY - 1):
        total = total + part_one[number]
    total_two[...] = total
    for number, peer in enumerate(row_peers):
        send(total_two, part_two.at[number], 1, peer)

    stage(2, 8, wide, one, two, wide)
    stage(3, 6, wide, two, wide, wide)
    snap[RESIDENT] = joined(wide, 3, 0, TILE).astype(jnp.bfloat16)
    stage(1, 4, wide, wide, one, wide)
    stage(2, 2, wide, one, two, wide)
    stage(3, 0, wide, two, wide, wide)
    snap[RESIDENT + 1] = joined(wide, 3, 0, TILE).astype(jnp.bfloat16)

    turn(snap, block, 3)
    fresh = lax.dot_general(
        block[48:64, :], block[...], (((1,), (1,)), ((), ())), preferred_element_type=jnp.float32
    ) * (1.0 / cells)
    late[...] = jnp.concatenate([fresh[14:15], fresh[15:16]], axis=1)
    for number, peer in enumerate(column_peers):
        send(late, late_one.at[number], 3, peer)

    for f in range(4):
        state_out[f] = joined(wide, f, 0, TILE)

    received(part_two, 1)
    total = total_two[...]
    for number in range(GX - 1):
        total = total + part_two[number]
    whole[core] = total
    partner = (gx, gy + 1 - 2 * core)
    swap = send(whole.at[core], whole.at[core], 2, partner)

    received(late_one, 3)
    late_total[...] = late[...] + jnp.sum(late_one[...], axis=0)
    for number, peer in enumerate(row_peers):
        send(late_total, late_two.at[number], 4, peer)

    swap.wait()
    folded = jnp.concatenate([whole[0], whole[1]], axis=0)
    gram = jnp.concatenate([pltpu.roll(folded, MODES, 1), folded], axis=0)
    row = lax.broadcasted_iota(jnp.int32, (MODES, TILE), 0)
    unit = (row >= RESIDENT) & (row == lanes((MODES, TILE)))
    early = inverse_factor(jnp.where(unit, 1.0, gram))
    inverse_out[...] = early

    received(late_two, 4)
    pair = late_total[...] + jnp.sum(late_two[...], axis=0)
    lane = lanes((1, TILE))
    first = jnp.where(lane < MODES, pair, 0.0)
    second = jnp.where(lane < MODES, pltpu.roll(pair, MODES, 1), 0.0)

    def pick(vector, place):
        return jnp.sum(jnp.where(lane == place, vector, 0.0), axis=1, keepdims=True)

    norm_first, norm_second, cross = pick(first, 62), pick(second, 63), pick(second, 62)
    known = lane < RESIDENT
    both = jnp.concatenate(
        [jnp.where(known, first, 0.0), jnp.where(known, second, 0.0), jnp.zeros((6, TILE), jnp.float32)], axis=0
    )
    along = exact_dot(both, early, ((1,), (1,)))
    back = exact_dot(along, early, ((1,), (0,)))
    along_first, along_second = along[0:1], along[1:2]
    scale_first = 1.0 / jnp.sqrt(norm_first - jnp.sum(along_first * along_first, axis=1, keepdims=True))
    row_first = (jnp.where(lane == 62, 1.0, 0.0) - back[0:1]) * scale_first
    shared = (cross - jnp.sum(along_first * along_second, axis=1, keepdims=True)) * scale_first
    left = norm_second - jnp.sum(along_second * along_second, axis=1, keepdims=True) - shared * shared
    row_second = (jnp.where(lane == 63, 1.0, 0.0) - back[1:2] - shared * row_first) * (1.0 / jnp.sqrt(left))
    inverse_out[62:63, :] = row_first
    inverse_out[63:64, :] = row_second

    sent(part_one, 0)
    sent(part_two, 1)
    sent(late_one, 3)
    sent(late_two, 4)


def basis_kernel(inverse_ref, block_ref, state_hbm, basis_hbm, state_out, basis, sem, state_sem):
    move = pltpu.make_async_copy(state_hbm, state_out, state_sem)
    move.start()
    inverse = inverse_ref[:, :MODES]
    high = inverse.astype(jnp.bfloat16)
    rest = inverse - high.astype(jnp.float32)
    middle = rest.astype(jnp.bfloat16)
    low = (rest - middle.astype(jnp.float32)).astype(jnp.bfloat16)
    weight = jnp.concatenate([high, middle, low], axis=1)
    copies = []
    for start in range(0, TILE, 8):
        part = block_ref[:, start * TILE : (start + 8) * TILE]
        rows = jnp.dot(weight, jnp.concatenate([part, part, part], axis=0), preferred_element_type=jnp.float32)
        stacked = jnp.stack([rows[:, i * TILE : (i + 1) * TILE] for i in range(8)], axis=0)
        here = pl.ds(start, 8)
        basis[:, here, :] = jnp.swapaxes(stacked, 0, 1)
        copies.append(pltpu.make_async_copy(basis.at[:, here, :], basis_hbm.at[:, here, :], sem.at[start // 8]))
        copies[-1].start()
    for copy in copies:
        copy.wait()
    move.wait()


def first(flow_state, sound_speed_sq, snapshots):
    hbm = pl.BlockSpec(memory_space=pltpu.HBM)
    local = pl.BlockSpec(memory_space=pltpu.VMEM)
    f32, bf16 = jnp.float32, jnp.bfloat16
    wide = pltpu.VMEM((2, 4, ROWS, TILE), f32)
    return pl.pallas_call(
        wide_kernel,
        out_shape=(
            jax.ShapeDtypeStruct((4, TILE, TILE), f32),
            jax.ShapeDtypeStruct((MODES, TILE * TILE), bf16),
            jax.ShapeDtypeStruct((MODES, TILE), f32),
        ),
        in_specs=[hbm] * 3,
        out_specs=(local, local, local),
        scratch_shapes=[
            pltpu.VMEM((MODES, TILE, TILE), bf16),
            pltpu.VMEM((FIELDS, ROWS, TILE), f32),
            pltpu.VMEM((2, FIELDS, ROWS, TILE), f32),
            wide,
            wide,
            pltpu.VMEM((TILE, TILE), f32),
            pltpu.VMEM((ROWS, TILE), f32),
            pltpu.VMEM((ROWS, TILE), f32),
            pltpu.VMEM((2, 16, TILE), f32),
            pltpu.VMEM((GY - 1, 16, TILE), f32),
            pltpu.VMEM((GX - 1, 16, TILE), f32),
            pltpu.VMEM((16, TILE), f32),
            pltpu.VMEM((2, 16, TILE), f32),
            pltpu.VMEM((1, TILE), f32),
            pltpu.VMEM((GY - 1, 1, TILE), f32),
            pltpu.VMEM((GX - 1, 1, TILE), f32),
            pltpu.VMEM((1, TILE), f32),
            pltpu.SemaphoreType.DMA((3,)),
            pltpu.SemaphoreType.DMA((8,)),
            pltpu.SemaphoreType.DMA((8,)),
            pltpu.SemaphoreType.DMA((5,)),
            pltpu.SemaphoreType.DMA((5,)),
        ],
        compiler_params=pltpu.CompilerParams(
            collective_id=0, has_side_effects=True, vmem_limit_bytes=40 << 20
        ),
        name="flow_and_gram",
    )(*(pltpu.with_memory_space_constraint(x, pltpu.HBM) for x in (flow_state, sound_speed_sq, snapshots)))


def body(flow_state, sound_speed_sq, snapshots):
    new_state, block, inverse = first(flow_state, sound_speed_sq, snapshots)
    local = pl.BlockSpec(memory_space=pltpu.VMEM)
    anywhere = pl.BlockSpec(memory_space=pl.ANY)
    hbm = pl.BlockSpec(memory_space=pltpu.HBM)
    f32 = jnp.float32
    pod_basis, new_state = pl.pallas_call(
        basis_kernel,
        out_shape=(
            jax.ShapeDtypeStruct((MODES, TILE, TILE), f32),
            jax.ShapeDtypeStruct((4, TILE, TILE), f32),
        ),
        in_specs=[local, local, anywhere],
        out_specs=(hbm, hbm),
        scratch_shapes=[
            pltpu.VMEM((MODES, TILE, TILE), f32),
            pltpu.SemaphoreType.DMA((TILE // 8,)),
            pltpu.SemaphoreType.DMA,
        ],
        compiler_params=pltpu.CompilerParams(vmem_limit_bytes=20 << 20),
        name="basis",
    )(inverse, block, new_state)
    return new_state, pod_basis


def solution(mesh):
    placed = (P(None, "gx", "gy"), P("gx", "gy"), P(None, "gx", "gy"))
    return jax.shard_map(
        body,
        mesh=mesh,
        in_specs=placed,
        out_specs=(P(None, "gx", "gy"), P(None, "gx", "gy")),
        check_vma=False,
    )
```

time: 57.2 us -> 35.4 us (0.62)
  the two profiles are of different devices: /device:TPU:1 before, /device:TPU:16 now
where the time goes in v2:
time: 35.4 us; the launch traced here: 35.3 us
  Pallas kernels  34.7 us (98%)
  between operations  0.64 us (2%)
    pallas_call x1, Pallas kernels, first(): pl.pallas_call(wide_kernel, out_shape=(jax.ShapeDtypeStruct((4, TILE, TIL...  32.2 us
    pallas_call x1, Pallas kernels, body(): pl.pallas_call(basis_kernel, out_shape=(jax.ShapeDtypeStruct((MODES, TILE...  2.54 us

profile of v2, /device:TPU:16, one launch (start us, length us, event | category | flops | bytes accessed | tf_op | source)
XLA Modules:
  0.0 35.3 jit_solution(758021751692511368)
XLA Ops:
  0.6 32.2 %flow_and_gram.1 = (f32[4,128,128]{2,1,0:T(8,128)S(1)}, bf16[64,16384]{1,0:T(8,128)(2,1)S(1)}, f32[64,128]{1,0:T(8,128)S(1)}) custom-call(f32[4,128,128]{2,1,0:T(8,128)} %flow_hbm.1, f32[128,128]{1,0:T(8,128)} %sound_hbm.1, bf16[62,128,128]{2,1,0:T(8,128)(2,1)} %snap_hbm.1), custom_call_target="tpu_custom_call" | custom-call | tf_op jit(solution)/shard_map/flow_and_gram/pallas_call | solution.py:341
  32.8 2.5 %basis.1 = (f32[64,128,128]{2,1,0:T(8,128)}, f32[4,128,128]{2,1,0:T(8,128)}) custom-call(f32[64,128]{1,0:T(8,128)S(1)} %get-tuple-element.7.inverse_ref, bf16[64,16384]{1,0:T(8,128)(2,1)S(1)} %get-tuple-element.8.block_ref, f32[4,128,128]{2,1,0:T(8,128)S(1)} %get-tuple-element.9.state_hbm), custom_call_target="tpu_custom_call" | custom-call | tf_op jit(solution)/shard_map/basis/pallas_call | solution.py:387

commit v3 on v2

--- a/solution.py
+++ b/solution.py
@@ -38,14 +38,34 @@
     return 8.0 * near - far
 
 
-def stage(kind, margin, state, source, target, sound):
-    rows, scale = 8, courant / 12.0
-    for row in range(PAD - margin, PAD + TILE + margin, rows):
+def lane_band():
+    away = lax.rem(
+        lax.broadcasted_iota(jnp.int32, (TILE, TILE), 0) - lanes((TILE, TILE)) + TILE, TILE
+    )
+    band = jnp.where(away == 1, 8.0, jnp.where(away == TILE - 1, -8.0, 0.0))
+    band = jnp.where(away == 2, -1.0, jnp.where(away == TILE - 2, 1.0, band)).astype(jnp.bfloat16)
+    return jnp.concatenate([band, band, band], axis=0)
+
+
+def split(value):
+    high = value.astype(jnp.bfloat16)
+    rest = value - high.astype(jnp.float32)
+    middle = rest.astype(jnp.bfloat16)
+    return [high, middle, (rest - middle.astype(jnp.float32)).astype(jnp.bfloat16)]
+
+
+def stage(kind, margin, state, source, target, sound, band):
+    scale = courant / 12.0
+    row, end = PAD - margin, PAD + TILE + margin
+    while row < end:
+        rows = 16 if end - row > 8 else 8
         here = pl.ds(row, rows)
         for w in range(2):
             centre = [source[w, f, here, :] for f in range(4)]
             dx = [slope_rows(source, w, f, row, rows) for f in range(4)]
-            dy = [slope_lanes(centre[f]) for f in range(4)]
+            pair = jnp.concatenate(split(jnp.concatenate(centre[2:], axis=0)), axis=1)
+            pair = jnp.dot(pair, band, preferred_element_type=jnp.float32)
+            dy = [slope_lanes(centre[0]), slope_lanes(centre[1]), pair[:rows], pair[rows:]]
             diverge = dx[1] + dy[2]
             advect = [stream_speed * dx[f] + span_speed * dy[f] for f in range(4)]
             rate = [
@@ -64,6 +84,7 @@
                         (2.0 / 3.0) * centre[f] - (2.0 / 3.0 * scale) * rate[f]
                     )
                 target[w, f, here, :] = moved
+        row += rows
 
 
 def joined(wide, field, row, rows):
@@ -128,8 +149,8 @@
     flow_hbm, sound_hbm, snap_hbm, state_out, block, inverse_out,
     snap, tile, wide, one, two, strip, left_strip, right_strip,
     packed, part_one, part_two, total_two, whole,
-    late, late_one, late_two, late_total,
-    load_sem, halo_send, halo_recv, sum_send, sum_recv,
+    line, late, late_one, late_two, late_total,
+    reach_sem, load_sem, halo_send, halo_recv, sum_send, sum_recv,
 ):
     gx, gy = lax.axis_index("gx"), lax.axis_index("gy")
     core = lax.rem(gy, 2)
@@ -138,13 +159,26 @@
     def at(dx, dy):
         return (lax.rem(gx + (dx + GX), GX), lax.rem(gy + (dy + GY), GY))
 
-    row_peers = [at(d, 0) for d in range(1, GX)]
-    column_peers = [at(0, d) for d in range(1, GY)]
+    x, z, y = gx // 8, lax.rem(gx, 8), gy // 2
+    row_steps = sorted(
+        ((dx, dz) for dx in range(4) for dz in range(8) if dx or dz),
+        key=lambda step: -min(step[0], 4 - step[0]) - min(step[1], 8 - step[1]),
+    )
+    row_peers = [(lax.rem(x + dx, 4) * 8 + lax.rem(z + dz, 8), gy) for dx, dz in row_steps]
+    column_steps = sorted(
+        ((dy, dc) for dy in range(4) for dc in range(2) if dy or dc), key=lambda step: -min(step[0], 4 - step[0])
+    )
+    column_peers = [(gx, lax.rem(y + dy, 4) * 2 + lax.rem(core + dc, 2)) for dy, dc in column_steps]
     corner_peers = [at(dx, dy) for dx in (-1, 1) for dy in (-1, 1)]
-    everyone = row_peers + column_peers + corner_peers
+    near_peers = [
+        peer
+        for (dx, dz), peer in zip(row_steps, row_peers)
+        if min(dx, 4 - dx) <= 1 and min(dz, 8 - dz) <= 2
+    ]
+    entered = near_peers + column_peers + corner_peers
 
     barrier = pltpu.get_barrier_semaphore()
-    for peer in everyone:
+    for peer in entered:
         pl.semaphore_signal(barrier, inc=1, device_id=peer, device_id_type=MESH)
 
     inside = pl.ds(PAD, TILE)
@@ -155,6 +189,7 @@
     ]
     for load in loads:
         load.start()
+    line[...] = jnp.zeros((TILE, 8, TILE), jnp.float32)
     snap[RESIDENT:MODES] = jnp.zeros((MODES - RESIDENT, TILE, TILE), jnp.bfloat16)
     loads[0].wait()
     loads[1].wait()
@@ -170,14 +205,7 @@
     loads[2].wait()
     for group in range(4):
         turn(snap, block, group)
-    gram = lax.dot_general(
-        block[...], block[...], (((1,), (1,)), ((), ())), preferred_element_type=jnp.float32
-    ) * (1.0 / cells)
-    folded = jnp.concatenate([gram[32:64], gram[0:32]], axis=1)
-    packed[0] = folded[0:16]
-    packed[1] = folded[16:32]
-
-    pl.semaphore_wait(barrier, len(everyone))
+    pl.semaphore_wait(barrier, len(entered))
 
     top, bottom = pl.ds(0, PAD), pl.ds(PAD + TILE, PAD)
     low, high = pl.ds(0, PAD), pl.ds(TILE - PAD, PAD)
@@ -215,6 +243,16 @@
     def sent(ref, slot):
         pltpu.make_async_copy(ref, ref, sum_send.at[slot]).wait()
 
+    for peer in near_peers:
+        pl.semaphore_signal(reach_sem, inc=1, device_id=peer, device_id_type=MESH)
+
+    gram = lax.dot_general(
+        block[...], block[...], (((1,), (1,)), ((), ())), preferred_element_type=jnp.float32
+    ) * (1.0 / cells)
+    folded = jnp.concatenate([gram[32:64], gram[0:32]], axis=1)
+    packed[0] = folded[0:16]
+    packed[1] = folded[16:32]
+
     for number, peer in enumerate(column_peers):
         send(packed.at[lax.rem(peer[1], 2)], part_one.at[number], 0, peer)
 
@@ -229,34 +267,55 @@
             wide[0, f, here, :] = jnp.where(lane < HALO, beside, turned)
             wide[1, f, here, :] = jnp.where((lane >= HALO) & (lane < 2 * HALO), beside, turned)
 
-    stage(1, 10, wide, wide, one, wide)
+    band = lane_band()
+    stage(1, 10, wide, wide, one, wide, band)
 
     received(part_one, 0)
     total = packed[core]
     for number in range(GY - 1):
         total = total + part_one[number]
     total_two[...] = total
+    pl.semaphore_wait(reach_sem, len(near_peers))
     for number, peer in enumerate(row_peers):
         send(total_two, part_two.at[number], 1, peer)
 
-    stage(2, 8, wide, one, two, wide)
-    stage(3, 6, wide, two, wide, wide)
-    snap[RESIDENT] = joined(wide, 3, 0, TILE).astype(jnp.bfloat16)
-    stage(1, 4, wide, wide, one, wide)
-    stage(2, 2, wide, one, two, wide)
-    stage(3, 0, wide, two, wide, wide)
-    snap[RESIDENT + 1] = joined(wide, 3, 0, TILE).astype(jnp.bfloat16)
-
-    turn(snap, block, 3)
-    fresh = lax.dot_general(
-        block[48:64, :], block[...], (((1,), (1,)), ((), ())), preferred_element_type=jnp.float32
-    ) * (1.0 / cells)
-    late[...] = jnp.concatenate([fresh[14:15], fresh[15:16]], axis=1)
+    stage(2, 8, wide, one, two, wide, band)
+    stage(3, 6, wide, two, wide, wide, band)
+    pressures = [joined(wide, 3, 0, TILE).astype(jnp.bfloat16)]
+    snap[RESIDENT] = pressures[0]
+    pressures[0] = pressures[0].astype(jnp.float32)
+    line[:, 0, :] = pressures[0]
+    stage(1, 4, wide, wide, one, wide, band)
+    stage(2, 2, wide, one, two, wide, band)
+    stage(3, 0, wide, two, wide, wide, band)
+    pressures.append(joined(wide, 3, 0, TILE).astype(jnp.bfloat16))
+    snap[RESIDENT + 1] = pressures[1]
+    pressures[1] = pressures[1].astype(jnp.float32)
+    line[:, 1, :] = pressures[1]
+
+    flat = jnp.concatenate([line[i].astype(jnp.bfloat16) for i in range(TILE)], axis=1)
+    fresh = lax.dot_general(flat, block[...], (((1,), (1,)), ((), ())), preferred_element_type=jnp.float32)
+
+    def product(a, b):
+        return jnp.sum(jnp.sum(pressures[a] * pressures[b], axis=0, keepdims=True), axis=1, keepdims=True)
+
+    pair = jnp.concatenate([fresh[0:1], fresh[1:2]], axis=1)
+    place = lanes((1, TILE))
+    for where, value in ((62, product(0, 0)), (126, product(0, 1)), (127, product(1, 1))):
+        pair = jnp.where(place == where, value, pair)
+    late[...] = pair * (1.0 / cells)
     for number, peer in enumerate(column_peers):
         send(late, late_one.at[number], 3, peer)
 
+    turn(snap, block, 3)
+
     for f in range(4):
         state_out[f] = joined(wide, f, 0, TILE)
+
+    received(late_one, 3)
+    late_total[...] = late[...] + jnp.sum(late_one[...], axis=0)
+    for number, peer in enumerate(row_peers):
+        send(late_total, late_two.at[number], 4, peer)
 
     received(part_two, 1)
     total = total_two[...]
@@ -266,11 +325,6 @@
     partner = (gx, gy + 1 - 2 * core)
     swap = send(whole.at[core], whole.at[core], 2, partner)
 
-    received(late_one, 3)
-    late_total[...] = late[...] + jnp.sum(late_one[...], axis=0)
-    for number, peer in enumerate(row_peers):
-        send(late_total, late_two.at[number], 4, peer)
-
     swap.wait()
     folded = jnp.concatenate([whole[0], whole[1]], axis=0)
     gram = jnp.concatenate([pltpu.roll(folded, MODES, 1), folded], axis=0)
@@ -278,6 +332,7 @@
     unit = (row >= RESIDENT) & (row == lanes((MODES, TILE)))
     early = inverse_factor(jnp.where(unit, 1.0, gram))
     inverse_out[...] = early
+    normal = exact_dot(early, early, ((0,), (0,)))
 
     received(late_two, 4)
     pair = late_total[...] + jnp.sum(late_two[...], axis=0)
@@ -294,7 +349,7 @@
         [jnp.where(known, first, 0.0), jnp.where(known, second, 0.0), jnp.zeros((6, TILE), jnp.float32)], axis=0
     )
     along = exact_dot(both, early, ((1,), (1,)))
-    back = exact_dot(along, early, ((1,), (0,)))
+    back = exact_dot(both, normal, ((1,), (0,)))
     along_first, along_second = along[0:1], along[1:2]
     scale_first = 1.0 / jnp.sqrt(norm_first - jnp.sum(along_first * along_first, axis=1, keepdims=True))
     row_first = (jnp.where(lane == 62, 1.0, 0.0) - back[0:1]) * scale_first
@@ -361,10 +416,12 @@
             pltpu.VMEM((GX - 1, 16, TILE), f32),
             pltpu.VMEM((16, TILE), f32),
             pltpu.VMEM((2, 16, TILE), f32),
+            pltpu.VMEM((TILE, 8, TILE), f32),
             pltpu.VMEM((1, TILE), f32),
             pltpu.VMEM((GY - 1, 1, TILE), f32),
             pltpu.VMEM((GX - 1, 1, TILE), f32),
             pltpu.VMEM((1, TILE), f32),
+            pltpu.SemaphoreType.REGULAR,
             pltpu.SemaphoreType.DMA((3,)),
             pltpu.SemaphoreType.DMA((8,)),
             pltpu.SemaphoreType.DMA((8,)),

time: 35.4 us -> 32.4 us (0.915)
  the two profiles are of different devices: /device:TPU:16 before, /device:TPU:1 now
where the time goes in v3:
time: 32.4 us; the launch traced here: 32.3 us
  Pallas kernels  31.6 us (98%)
  between operations  0.64 us (2%)
    pallas_call x1, Pallas kernels, first(): pl.pallas_call(wide_kernel, out_shape=(jax.ShapeDtypeStruct((4, TILE, TIL...  29.1 us
    pallas_call x1, Pallas kernels, body(): pl.pallas_call(basis_kernel, out_shape=(jax.ShapeDtypeStruct((MODES, TILE...  2.55 us

profile of v3, /device:TPU:1, one launch (start us, length us, event | category | flops | bytes accessed | tf_op | source)
XLA Modules:
  0.0 32.3 jit_solution(13140594028272956519)
XLA Ops:
  0.6 29.1 %flow_and_gram.1 = (f32[4,128,128]{2,1,0:T(8,128)S(1)}, bf16[64,16384]{1,0:T(8,128)(2,1)S(1)}, f32[64,128]{1,0:T(8,128)S(1)}) custom-call(f32[4,128,128]{2,1,0:T(8,128)} %flow_hbm.1, f32[128,128]{1,0:T(8,128)} %sound_hbm.1, bf16[62,128,128]{2,1,0:T(8,128)(2,1)} %snap_hbm.1), custom_call_target="tpu_custom_call" | custom-call | tf_op jit(solution)/shard_map/flow_and_gram/pallas_call | solution.py:396
  29.7 2.5 %basis.1 = (f32[64,128,128]{2,1,0:T(8,128)}, f32[4,128,128]{2,1,0:T(8,128)}) custom-call(f32[64,128]{1,0:T(8,128)S(1)} %get-tuple-element.7.inverse_ref, bf16[64,16384]{1,0:T(8,128)(2,1)S(1)} %get-tuple-element.8.block_ref, f32[4,128,128]{2,1,0:T(8,128)S(1)} %get-tuple-element.9.state_hbm), custom_call_target="tpu_custom_call" | custom-call | tf_op jit(solution)/shard_map/basis/pallas_call | solution.py:444

commit v4 on v3

--- a/solution.py
+++ b/solution.py
@@ -14,6 +14,7 @@
 MODES = 64
 RESIDENT = 62
 TILE = 128
+EARLY_ROWS = 64
 HALO = 12
 PAD = 16
 ROWS = TILE + 2 * PAD
@@ -112,17 +113,25 @@
             for j in range(8)
             for r in range(t, count)
         }
-        for j in range(8):
-            inverse_pivot = 1.0 / spread(column[j, t][j : j + 1, :])
-            factor = {r: column[j, r] * inverse_pivot for r in range(t, count)}
-            factor[t] = jnp.where(sub > j, factor[t], 0.0)
-            for later in range(j + 1, 8):
-                entry = spread(column[later, t][j : j + 1, :])
+        for j in range(0, 8, 2):
+            corner, side = spread(column[j, t][j : j + 1, :]), spread(column[j + 1, t][j : j + 1, :])
+            below, other = spread(column[j, t][j + 1 : j + 2, :]), spread(column[j + 1, t][j + 1 : j + 2, :])
+            inverse_first = 1.0 / corner
+            inverse_second = corner * (1.0 / (corner * other - below * side))
+            ratio = below * inverse_first
+            first = {r: column[j, r] * inverse_first for r in range(t, count)}
+            first[t] = jnp.where(sub > j, first[t], 0.0)
+            second = {r: (column[j + 1, r] - first[r] * side) * inverse_second for r in range(t, count)}
+            second[t] = jnp.where(sub > j + 1, second[t], 0.0)
+            for later in range(j + 2, 8):
+                upper = spread(column[later, t][j : j + 1, :])
+                lower = spread(column[later, t][j + 1 : j + 2, :]) - ratio * upper
                 for r in range(t, count):
-                    column[later, r] = column[later, r] - factor[r] * entry
-            pivot_row = spread(tiles[t][j : j + 1, :])
+                    column[later, r] = column[later, r] - first[r] * upper - second[r] * lower
+            upper = spread(tiles[t][j : j + 1, :])
+            lower = spread(tiles[t][j + 1 : j + 2, :]) - ratio * upper
             for r in range(t, count):
-                tiles[r] = tiles[r] - factor[r] * pivot_row
+                tiles[r] = tiles[r] - first[r] * upper - second[r] * lower
     rows = []
     for r in range(count):
         diagonal = jnp.sum(jnp.where(lane == 8 * r + sub, tiles[r], 0.0), axis=1, keepdims=True)
@@ -131,24 +140,51 @@
     return jnp.concatenate(rows, axis=0)
 
 
+def fold(gram):
+    half = MODES // 2
+    wide = jnp.concatenate([gram, jnp.zeros_like(gram)], axis=1)
+    early, late = wide[:half], wide[half:]
+    row, lane = lax.broadcasted_iota(jnp.int32, (half, TILE), 0), lanes((half, TILE))
+    diagonal = jnp.sum(jnp.where(lane == row + half, late, 0.0), axis=0, keepdims=True)
+    mixed = jnp.where((lane >= half) & (lane <= row + half), pltpu.roll(early, half, 1), late)
+    mixed = jnp.where((row == RESIDENT - half) & (lane < half), pltpu.roll(diagonal, TILE - half, 1), mixed)
+    return mixed[: half // 2] + pltpu.roll(mixed[half // 2 :], MODES, 1)
+
+
+def unfold(folded):
+    half = MODES // 2
+    row, lane = lax.broadcasted_iota(jnp.int32, (half, TILE), 0), lanes((half, TILE))
+    mixed = jnp.concatenate([folded, pltpu.roll(folded, MODES, 1)], axis=0)
+    diagonal = pltpu.roll(mixed[RESIDENT - half : RESIDENT - half + 1], half, 1)
+    empty = (lane >= MODES) | ((lane < half) & (row >= RESIDENT - half))
+    mixed = jnp.where(empty, 0.0, mixed)
+    early = jnp.where(lane <= row, pltpu.roll(mixed, TILE - half, 1), 0.0)
+    late = jnp.where((lane < half) | (lane > row + half), mixed, 0.0)
+    whole = jnp.concatenate([early, late], axis=0)
+    turned = jnp.concatenate([whole[:, :MODES].T, jnp.zeros((MODES, MODES), jnp.float32)], axis=1)
+    row, lane = lax.broadcasted_iota(jnp.int32, (MODES, TILE), 0), lanes((MODES, TILE))
+    middle = jnp.where(row < half, whole, jnp.where(row < RESIDENT, diagonal, 1.0))
+    return jnp.where(row == lane, middle, whole + turned)
+
+
 def exact_dot(a, b, contract):
     return lax.dot_general(
         a, b, (contract, ((), ())), precision=lax.Precision.HIGHEST, preferred_element_type=jnp.float32
     )
 
 
-def turn(snap, block, group):
+def turn(snap, block, group, first=0, last=TILE):
     modes = pl.ds(group * 16, 16)
-    for row in range(0, TILE, 16):
+    for row in range(first, last, 16):
         turned = jnp.swapaxes(snap[modes, row : row + 16, :], 0, 1)
         for i in range(16):
             block[modes, (row + i) * TILE : (row + i + 1) * TILE] = turned[i]
 
 
 def wide_kernel(
-    flow_hbm, sound_hbm, snap_hbm, state_out, block, inverse_out,
+    flow_hbm, sound_hbm, snap_hbm, state_out, block, inverse_out, normal_out, late_out,
     snap, tile, wide, one, two, strip, left_strip, right_strip,
-    packed, part_one, part_two, total_two, whole,
+    packed, part_one, part_two, total_two,
     line, late, late_one, late_two, late_total,
     reach_sem, load_sem, halo_send, halo_recv, sum_send, sum_recv,
 ):
@@ -173,7 +209,7 @@
     near_peers = [
         peer
         for (dx, dz), peer in zip(row_steps, row_peers)
-        if min(dx, 4 - dx) <= 1 and min(dz, 8 - dz) <= 2
+        if min(dx, 4 - dx) + min(dz, 8 - dz) <= 2
     ]
     entered = near_peers + column_peers + corner_peers
 
@@ -185,7 +221,13 @@
     loads = [
         pltpu.make_async_copy(flow_hbm, tile.at[pl.ds(0, 4), inside, :], load_sem.at[0]),
         pltpu.make_async_copy(sound_hbm, tile.at[4, inside, :], load_sem.at[1]),
-        pltpu.make_async_copy(snap_hbm, snap.at[pl.ds(0, RESIDENT)], load_sem.at[2]),
+    ] + [
+        pltpu.make_async_copy(
+            snap_hbm.at[:, pl.ds(part * 32, 32), :],
+            snap.at[pl.ds(0, RESIDENT), pl.ds(part * 32, 32), :],
+            load_sem.at[2 + part],
+        )
+        for part in range(4)
     ]
     for load in loads:
         load.start()
@@ -202,9 +244,19 @@
             gathered = jnp.where(lane >= 24 * f, moved, gathered)
         strip[pl.ds(row, 16), :] = gathered
 
-    loads[2].wait()
-    for group in range(4):
-        turn(snap, block, group)
+    def products(first, last, so_far):
+        for row in range(first, last, 16):
+            if row % 32 == 0:
+                loads[2 + row // 32].wait()
+            for group in range(4):
+                turn(snap, block, group, row, row + 16)
+            piece = block[:, row * TILE : (row + 16) * TILE]
+            so_far = so_far + lax.dot_general(
+                piece, piece, (((1,), (1,)), ((), ())), preferred_element_type=jnp.float32
+            )
+        return so_far
+
+    gram = products(0, EARLY_ROWS, jnp.zeros((MODES, MODES), jnp.float32))
     pl.semaphore_wait(barrier, len(entered))
 
     top, bottom = pl.ds(0, PAD), pl.ds(PAD + TILE, PAD)
@@ -243,19 +295,20 @@
     def sent(ref, slot):
         pltpu.make_async_copy(ref, ref, sum_send.at[slot]).wait()
 
-    for peer in near_peers:
-        pl.semaphore_signal(reach_sem, inc=1, device_id=peer, device_id_type=MESH)
-
-    gram = lax.dot_general(
-        block[...], block[...], (((1,), (1,)), ((), ())), preferred_element_type=jnp.float32
-    ) * (1.0 / cells)
-    folded = jnp.concatenate([gram[32:64], gram[0:32]], axis=1)
-    packed[0] = folded[0:16]
-    packed[1] = folded[16:32]
+    def pass_on(step):
+        for peer in near_peers:
+            pl.semaphore_signal(reach_sem.at[step], inc=1, device_id=peer, device_id_type=MESH)
+
+    pass_on(0)
+
+    gram = products(EARLY_ROWS, TILE, gram) * (1.0 / cells)
+    packed[...] = fold(gram)
 
     for number, peer in enumerate(column_peers):
-        send(packed.at[lax.rem(peer[1], 2)], part_one.at[number], 0, peer)
-
+        send(packed, part_one.at[number], 0, peer)
+
+    pl.semaphore_wait(reach_sem.at[0], len(near_peers))
+    pass_on(1)
     for halo in halos:
         halo.wait()
     for row in range(0, ROWS, 16):
@@ -271,11 +324,11 @@
     stage(1, 10, wide, wide, one, wide, band)
 
     received(part_one, 0)
-    total = packed[core]
+    total = packed[...]
     for number in range(GY - 1):
         total = total + part_one[number]
     total_two[...] = total
-    pl.semaphore_wait(reach_sem, len(near_peers))
+    pl.semaphore_wait(reach_sem.at[1], len(near_peers))
     for number, peer in enumerate(row_peers):
         send(total_two, part_two.at[number], 1, peer)
 
@@ -321,21 +374,21 @@
     total = total_two[...]
     for number in range(GX - 1):
         total = total + part_two[number]
-    whole[core] = total
-    partner = (gx, gy + 1 - 2 * core)
-    swap = send(whole.at[core], whole.at[core], 2, partner)
-
-    swap.wait()
-    folded = jnp.concatenate([whole[0], whole[1]], axis=0)
-    gram = jnp.concatenate([pltpu.roll(folded, MODES, 1), folded], axis=0)
-    row = lax.broadcasted_iota(jnp.int32, (MODES, TILE), 0)
-    unit = (row >= RESIDENT) & (row == lanes((MODES, TILE)))
-    early = inverse_factor(jnp.where(unit, 1.0, gram))
+
+    early = inverse_factor(unfold(total))
     inverse_out[...] = early
-    normal = exact_dot(early, early, ((0,), (0,)))
+    normal_out[...] = exact_dot(early, early, ((0,), (0,)))
 
     received(late_two, 4)
-    pair = late_total[...] + jnp.sum(late_two[...], axis=0)
+    late_out[...] = late_total[...] + jnp.sum(late_two[...], axis=0)
+
+    sent(part_one, 0)
+    sent(part_two, 1)
+    sent(late_one, 3)
+    sent(late_two, 4)
+
+
+def last_rows(early, normal, pair):
     lane = lanes((1, TILE))
     first = jnp.where(lane < MODES, pair, 0.0)
     second = jnp.where(lane < MODES, pltpu.roll(pair, MODES, 1), 0.0)
@@ -356,36 +409,41 @@
     shared = (cross - jnp.sum(along_first * along_second, axis=1, keepdims=True)) * scale_first
     left = norm_second - jnp.sum(along_second * along_second, axis=1, keepdims=True) - shared * shared
     row_second = (jnp.where(lane == 63, 1.0, 0.0) - back[1:2] - shared * row_first) * (1.0 / jnp.sqrt(left))
-    inverse_out[62:63, :] = row_first
-    inverse_out[63:64, :] = row_second
-
-    sent(part_one, 0)
-    sent(part_two, 1)
-    sent(late_one, 3)
-    sent(late_two, 4)
-
-
-def basis_kernel(inverse_ref, block_ref, state_hbm, basis_hbm, state_out, basis, sem, state_sem):
-    move = pltpu.make_async_copy(state_hbm, state_out, state_sem)
-    move.start()
-    inverse = inverse_ref[:, :MODES]
-    high = inverse.astype(jnp.bfloat16)
-    rest = inverse - high.astype(jnp.float32)
-    middle = rest.astype(jnp.bfloat16)
-    low = (rest - middle.astype(jnp.float32)).astype(jnp.bfloat16)
-    weight = jnp.concatenate([high, middle, low], axis=1)
-    copies = []
-    for start in range(0, TILE, 8):
-        part = block_ref[:, start * TILE : (start + 8) * TILE]
+    return row_first, row_second
+
+
+AHEAD = 3
+KNOWN = 48
+
+
+def basis_kernel(
+    early_ref, normal_ref, late_ref, block_ref, state_hbm, basis_hbm, state_out, basis, sem, ahead_sem, state_sem
+):
+    def weights(rows):
+        return jnp.concatenate(split(rows[:, :MODES]), axis=1)
+
+    def slab(number, weight, first, signal):
+        part = block_ref[:, number * 8 * TILE : (number + 1) * 8 * TILE]
         rows = jnp.dot(weight, jnp.concatenate([part, part, part], axis=0), preferred_element_type=jnp.float32)
         stacked = jnp.stack([rows[:, i * TILE : (i + 1) * TILE] for i in range(8)], axis=0)
-        here = pl.ds(start, 8)
-        basis[:, here, :] = jnp.swapaxes(stacked, 0, 1)
-        copies.append(pltpu.make_async_copy(basis.at[:, here, :], basis_hbm.at[:, here, :], sem.at[start // 8]))
-        copies[-1].start()
+        modes, here = pl.ds(first, weight.shape[0]), pl.ds(number * 8, 8)
+        basis[modes, here, :] = jnp.swapaxes(stacked, 0, 1)
+        copy = pltpu.make_async_copy(basis.at[modes, here, :], basis_hbm.at[modes, here, :], signal)
+        copy.start()
+        return copy
+
+    early = early_ref[...]
+    known = weights(early[:KNOWN])
+    copies = [slab(number, known, 0, ahead_sem.at[number]) for number in range(AHEAD)]
+    row_first, row_second = last_rows(early, normal_ref[...], late_ref[...])
+    rest = weights(jnp.concatenate([early[KNOWN:RESIDENT], row_first, row_second], axis=0))
+    copies += [slab(number, rest, KNOWN, sem.at[number]) for number in range(AHEAD)]
+    every = jnp.concatenate([known, rest], axis=0)
+    copies += [slab(number, every, 0, sem.at[number]) for number in range(AHEAD, TILE // 8)]
+    copies.append(pltpu.make_async_copy(state_hbm, state_out, state_sem))
+    copies[-1].start()
     for copy in copies:
         copy.wait()
-    move.wait()
 
 
 def first(flow_state, sound_speed_sq, snapshots):
@@ -399,9 +457,11 @@
             jax.ShapeDtypeStruct((4, TILE, TILE), f32),
             jax.ShapeDtypeStruct((MODES, TILE * TILE), bf16),
             jax.ShapeDtypeStruct((MODES, TILE), f32),
+            jax.ShapeDtypeStruct((TILE, TILE), f32),
+            jax.ShapeDtypeStruct((1, TILE), f32),
         ),
         in_specs=[hbm] * 3,
-        out_specs=(local, local, local),
+        out_specs=(local,) * 5,
         scratch_shapes=[
             pltpu.VMEM((MODES, TILE, TILE), bf16),
             pltpu.VMEM((FIELDS, ROWS, TILE), f32),
@@ -411,18 +471,17 @@
             pltpu.VMEM((TILE, TILE), f32),
             pltpu.VMEM((ROWS, TILE), f32),
             pltpu.VMEM((ROWS, TILE), f32),
-            pltpu.VMEM((2, 16, TILE), f32),
+            pltpu.VMEM((16, TILE), f32),
             pltpu.VMEM((GY - 1, 16, TILE), f32),
             pltpu.VMEM((GX - 1, 16, TILE), f32),
             pltpu.VMEM((16, TILE), f32),
-            pltpu.VMEM((2, 16, TILE), f32),
             pltpu.VMEM((TILE, 8, TILE), f32),
             pltpu.VMEM((1, TILE), f32),
             pltpu.VMEM((GY - 1, 1, TILE), f32),
             pltpu.VMEM((GX - 1, 1, TILE), f32),
             pltpu.VMEM((1, TILE), f32),
-            pltpu.SemaphoreType.REGULAR,
-            pltpu.SemaphoreType.DMA((3,)),
+            pltpu.SemaphoreType.REGULAR((2,)),
+            pltpu.SemaphoreType.DMA((6,)),
             pltpu.SemaphoreType.DMA((8,)),
             pltpu.SemaphoreType.DMA((8,)),
             pltpu.SemaphoreType.DMA((5,)),
@@ -436,7 +495,7 @@
 
 
 def body(flow_state, sound_speed_sq, snapshots):
-    new_state, block, inverse = first(flow_state, sound_speed_sq, snapshots)
+    new_state, block, early, normal, late = first(flow_state, sound_speed_sq, snapshots)
     local = pl.BlockSpec(memory_space=pltpu.VMEM)
     anywhere = pl.BlockSpec(memory_space=pl.ANY)
     hbm = pl.BlockSpec(memory_space=pltpu.HBM)
@@ -447,16 +506,17 @@
             jax.ShapeDtypeStruct((MODES, TILE, TILE), f32),
             jax.ShapeDtypeStruct((4, TILE, TILE), f32),
         ),
-        in_specs=[local, local, anywhere],
+        in_specs=[local] * 4 + [anywhere],
         out_specs=(hbm, hbm),
         scratch_shapes=[
             pltpu.VMEM((MODES, TILE, TILE), f32),
             pltpu.SemaphoreType.DMA((TILE // 8,)),
+            pltpu.SemaphoreType.DMA((AHEAD,)),
             pltpu.SemaphoreType.DMA,
         ],
         compiler_params=pltpu.CompilerParams(vmem_limit_bytes=20 << 20),
         name="basis",
-    )(inverse, block, new_state)
+    )(early, normal, late, block, new_state)
     return new_state, pod_basis
 
 

time: 32.4 us -> 31.6 us (0.975)
  Pallas kernels: 31.6 us -> 30.8 us
    pallas_call x1, Pallas kernels: 29.1 us -> 27.7 us  [first(): pl.pallas_call(wide_kernel, out_shape=(jax.ShapeDtypeStruct((4, TILE, TIL...]
    pallas_call x1, Pallas kernels: 2.55 us -> 3.16 us  [body(): pl.pallas_call(basis_kernel, out_shape=(jax.ShapeDtypeStruct((MODES, TILE...]
where the time goes in v4:
time: 31.6 us; the launch traced here: 31.5 us
  Pallas kernels  30.8 us (97%)
  between operations  0.64 us (2%)
    pallas_call x1, Pallas kernels, first(): pl.pallas_call(wide_kernel, out_shape=(jax.ShapeDtypeStruct((4, TILE, TIL...  27.7 us
    pallas_call x1, Pallas kernels, body(): pl.pallas_call(basis_kernel, out_shape=(jax.ShapeDtypeStruct((MODES, TILE...  3.16 us

profile of v4, /device:TPU:1, one launch (start us, length us, event | category | flops | bytes accessed | tf_op | source)
XLA Modules:
  0.0 31.5 jit_solution(4373170352341459830)
XLA Ops:
  0.6 27.7 %flow_and_gram.1 = (f32[4,128,128]{2,1,0:T(8,128)S(1)}, bf16[64,16384]{1,0:T(8,128)(2,1)S(1)}, f32[64,128]{1,0:T(8,128)S(1)}, f32[128,128]{1,0:T(8,128)S(1)}, f32[1,128]{1,0:T(1,128)S(1)}) custom-call(f32[4,128,128]{2,1,0:T(8,128)} %flow_hbm.1, f32[128,128]{1,0:T(8,128)} %sound_hbm.1, bf16[62,128,128]{2,1,0:T(8,128)(2,1)} %snap_hbm.1), custom_call_target="tpu_custom_call" | custom-call | tf_op jit(solution)/shard_map/flow_and_gram/pallas_call | solution.py:454
  28.3 3.2 %basis.1 = (f32[64,128,128]{2,1,0:T(8,128)}, f32[4,128,128]{2,1,0:T(8,128)}) custom-call(f32[64,128]{1,0:T(8,128)S(1)} %get-tuple-element.9.early_ref, f32[128,128]{1,0:T(8,128)S(1)} %get-tuple-element.10.normal_ref, f32[1,128]{1,0:T(1,128)S(1)} %get-tuple-element.11.late_ref, bf16[64,16384]{1,0:T(8,128)(2,1)S(1)} %get-tuple-element.12.block_ref, ...), custom_call_target="tpu_custom_call" | custom-call | tf_op jit(solution)/shard_map/basis/pallas_call | solution.py:503

commit v5 on v4

--- a/solution.py
+++ b/solution.py
@@ -205,6 +205,14 @@
         ((dy, dc) for dy in range(4) for dc in range(2) if dy or dc), key=lambda step: -min(step[0], 4 - step[0])
     )
     column_peers = [(gx, lax.rem(y + dy, 4) * 2 + lax.rem(core + dc, 2)) for dy, dc in column_steps]
+    chip_steps = sorted(
+        ((dx, dy, dz) for dx in range(4) for dy in range(4) for dz in range(8) if dx or dy or dz),
+        key=lambda step: -min(step[0], 4 - step[0]) - min(step[1], 4 - step[1]) - min(step[2], 8 - step[2]),
+    )
+    chip_peers = [
+        (lax.rem(x + dx, 4) * 8 + lax.rem(z + dz, 8), lax.rem(y + dy, 4) * 2 + core) for dx, dy, dz in chip_steps
+    ]
+    partner = (gx, gy + 1 - 2 * core)
     corner_peers = [at(dx, dy) for dx in (-1, 1) for dy in (-1, 1)]
     near_peers = [
         peer
@@ -295,11 +303,11 @@
     def sent(ref, slot):
         pltpu.make_async_copy(ref, ref, sum_send.at[slot]).wait()
 
-    def pass_on(step):
-        for peer in near_peers:
+    def pass_on(step, peers):
+        for peer in peers:
             pl.semaphore_signal(reach_sem.at[step], inc=1, device_id=peer, device_id_type=MESH)
 
-    pass_on(0)
+    pass_on(0, near_peers)
 
     gram = products(EARLY_ROWS, TILE, gram) * (1.0 / cells)
     packed[...] = fold(gram)
@@ -308,7 +316,7 @@
         send(packed, part_one.at[number], 0, peer)
 
     pl.semaphore_wait(reach_sem.at[0], len(near_peers))
-    pass_on(1)
+    pass_on(1, near_peers)
     for halo in halos:
         halo.wait()
     for row in range(0, ROWS, 16):
@@ -329,6 +337,7 @@
         total = total + part_one[number]
     total_two[...] = total
     pl.semaphore_wait(reach_sem.at[1], len(near_peers))
+    pass_on(2, column_peers)
     for number, peer in enumerate(row_peers):
         send(total_two, part_two.at[number], 1, peer)
 
@@ -357,18 +366,17 @@
     for where, value in ((62, product(0, 0)), (126, product(0, 1)), (127, product(1, 1))):
         pair = jnp.where(place == where, value, pair)
     late[...] = pair * (1.0 / cells)
-    for number, peer in enumerate(column_peers):
-        send(late, late_one.at[number], 3, peer)
+    swap = send(late, late_one, 3, partner)
+
+    pl.semaphore_wait(reach_sem.at[2], len(column_peers))
+    swap.wait()
+    late_total[...] = late[...] + late_one[...]
+    for number, peer in enumerate(chip_peers):
+        send(late_total, late_two.at[number], 4, peer)
 
     turn(snap, block, 3)
-
     for f in range(4):
         state_out[f] = joined(wide, f, 0, TILE)
-
-    received(late_one, 3)
-    late_total[...] = late[...] + jnp.sum(late_one[...], axis=0)
-    for number, peer in enumerate(row_peers):
-        send(late_total, late_two.at[number], 4, peer)
 
     received(part_two, 1)
     total = total_two[...]
@@ -380,11 +388,15 @@
     normal_out[...] = exact_dot(early, early, ((0,), (0,)))
 
     received(late_two, 4)
-    late_out[...] = late_total[...] + jnp.sum(late_two[...], axis=0)
+    parts = [late_two[number] for number in range(8)]
+    for number in range(8, len(chip_peers)):
+        parts[number % 8] = parts[number % 8] + late_two[number]
+    while len(parts) > 1:
+        parts = [a + b for a, b in zip(parts[::2], parts[1::2])]
+    late_out[...] = late_total[...] + parts[0]
 
     sent(part_one, 0)
     sent(part_two, 1)
-    sent(late_one, 3)
     sent(late_two, 4)
 
 
@@ -412,34 +424,26 @@
     return row_first, row_second
 
 
-AHEAD = 3
-KNOWN = 48
-
-
 def basis_kernel(
-    early_ref, normal_ref, late_ref, block_ref, state_hbm, basis_hbm, state_out, basis, sem, ahead_sem, state_sem
+    early_ref, normal_ref, late_ref, block_ref, state_hbm, basis_hbm, state_out, basis, sem, state_sem
 ):
     def weights(rows):
         return jnp.concatenate(split(rows[:, :MODES]), axis=1)
 
-    def slab(number, weight, first, signal):
+    def slab(number, weight):
         part = block_ref[:, number * 8 * TILE : (number + 1) * 8 * TILE]
         rows = jnp.dot(weight, jnp.concatenate([part, part, part], axis=0), preferred_element_type=jnp.float32)
         stacked = jnp.stack([rows[:, i * TILE : (i + 1) * TILE] for i in range(8)], axis=0)
-        modes, here = pl.ds(first, weight.shape[0]), pl.ds(number * 8, 8)
-        basis[modes, here, :] = jnp.swapaxes(stacked, 0, 1)
-        copy = pltpu.make_async_copy(basis.at[modes, here, :], basis_hbm.at[modes, here, :], signal)
+        here = pl.ds(number * 8, 8)
+        basis[:, here, :] = jnp.swapaxes(stacked, 0, 1)
+        copy = pltpu.make_async_copy(basis.at[:, here, :], basis_hbm.at[:, here, :], sem.at[number])
         copy.start()
         return copy
 
     early = early_ref[...]
-    known = weights(early[:KNOWN])
-    copies = [slab(number, known, 0, ahead_sem.at[number]) for number in range(AHEAD)]
     row_first, row_second = last_rows(early, normal_ref[...], late_ref[...])
-    rest = weights(jnp.concatenate([early[KNOWN:RESIDENT], row_first, row_second], axis=0))
-    copies += [slab(number, rest, KNOWN, sem.at[number]) for number in range(AHEAD)]
-    every = jnp.concatenate([known, rest], axis=0)
-    copies += [slab(number, every, 0, sem.at[number]) for number in range(AHEAD, TILE // 8)]
+    weight = weights(jnp.concatenate([early[:RESIDENT], row_first, row_second], axis=0))
+    copies = [slab(number, weight) for number in range(TILE // 8)]
     copies.append(pltpu.make_async_copy(state_hbm, state_out, state_sem))
     copies[-1].start()
     for copy in copies:
@@ -477,10 +481,10 @@
             pltpu.VMEM((16, TILE), f32),
             pltpu.VMEM((TILE, 8, TILE), f32),
             pltpu.VMEM((1, TILE), f32),
-            pltpu.VMEM((GY - 1, 1, TILE), f32),
-            pltpu.VMEM((GX - 1, 1, TILE), f32),
             pltpu.VMEM((1, TILE), f32),
-            pltpu.SemaphoreType.REGULAR((2,)),
+            pltpu.VMEM((GX * GY // 2 - 1, 1, TILE), f32),
+            pltpu.VMEM((1, TILE), f32),
+            pltpu.SemaphoreType.REGULAR((3,)),
             pltpu.SemaphoreType.DMA((6,)),
             pltpu.SemaphoreType.DMA((8,)),
             pltpu.SemaphoreType.DMA((8,)),
@@ -511,7 +515,6 @@
         scratch_shapes=[
             pltpu.VMEM((MODES, TILE, TILE), f32),
             pltpu.SemaphoreType.DMA((TILE // 8,)),
-            pltpu.SemaphoreType.DMA((AHEAD,)),
             pltpu.SemaphoreType.DMA,
         ],
         compiler_params=pltpu.CompilerParams(vmem_limit_bytes=20 << 20),

time: 31.6 us -> 31.4 us (level)
  no operation moved by 1% of the time
where the time goes in v5:
time: 31.4 us; the launch traced here: 31.3 us
  Pallas kernels  30.7 us (98%)
  between operations  0.64 us (2%)
    pallas_call x1, Pallas kernels, first(): pl.pallas_call(wide_kernel, out_shape=(jax.ShapeDtypeStruct((4, TILE, TIL...  27.7 us
    pallas_call x1, Pallas kernels, body(): pl.pallas_call(basis_kernel, out_shape=(jax.ShapeDtypeStruct((MODES, TILE...  2.96 us

profile of v5, /device:TPU:1, one launch (start us, length us, event | category | flops | bytes accessed | tf_op | source)
XLA Modules:
  0.0 31.3 jit_solution(3008200172367239526)
XLA Ops:
  0.6 27.7 %flow_and_gram.1 = (f32[4,128,128]{2,1,0:T(8,128)S(1)}, bf16[64,16384]{1,0:T(8,128)(2,1)S(1)}, f32[64,128]{1,0:T(8,128)S(1)}, f32[128,128]{1,0:T(8,128)S(1)}, f32[1,128]{1,0:T(1,128)S(1)}) custom-call(f32[4,128,128]{2,1,0:T(8,128)} %flow_hbm.1, f32[128,128]{1,0:T(8,128)} %sound_hbm.1, bf16[62,128,128]{2,1,0:T(8,128)(2,1)} %snap_hbm.1), custom_call_target="tpu_custom_call" | custom-call | tf_op jit(solution)/shard_map/flow_and_gram/pallas_call | solution.py:458
  28.4 3.0 %basis.1 = (f32[64,128,128]{2,1,0:T(8,128)}, f32[4,128,128]{2,1,0:T(8,128)}) custom-call(f32[64,128]{1,0:T(8,128)S(1)} %get-tuple-element.9.early_ref, f32[128,128]{1,0:T(8,128)S(1)} %get-tuple-element.10.normal_ref, f32[1,128]{1,0:T(1,128)S(1)} %get-tuple-element.11.late_ref, bf16[64,16384]{1,0:T(8,128)(2,1)S(1)} %get-tuple-element.12.block_ref, ...), custom_call_target="tpu_custom_call" | custom-call | tf_op jit(solution)/shard_map/basis/pallas_call | solution.py:507

commit v6 on v5

--- a/solution.py
+++ b/solution.py
@@ -14,7 +14,7 @@
 MODES = 64
 RESIDENT = 62
 TILE = 128
-EARLY_ROWS = 64
+EARLY_ROWS = 96
 HALO = 12
 PAD = 16
 ROWS = TILE + 2 * PAD
@@ -317,14 +317,18 @@
 
     pl.semaphore_wait(reach_sem.at[0], len(near_peers))
     pass_on(1, near_peers)
+    for row in range(PAD, PAD + TILE, 16):
+        for f in range(FIELDS):
+            wide[0, f, pl.ds(row, 16), :] = pltpu.roll(tile[f, pl.ds(row, 16), :], HALO, 1)
     for halo in halos:
         halo.wait()
     for row in range(0, ROWS, 16):
         here = pl.ds(row, 16)
+        main = PAD <= row < PAD + TILE
         merged = jnp.where(lax.rem(lane, 24) >= HALO, right_strip[here, :], left_strip[here, :])
         for f in range(FIELDS):
             beside = pltpu.roll(merged, TILE - 24 * f, 1) if f else merged
-            turned = pltpu.roll(tile[f, here, :], HALO, 1)
+            turned = wide[0, f, here, :] if main else pltpu.roll(tile[f, here, :], HALO, 1)
             wide[0, f, here, :] = jnp.where(lane < HALO, beside, turned)
             wide[1, f, here, :] = jnp.where((lane >= HALO) & (lane < 2 * HALO), beside, turned)
 

time: 31.4 us -> 31.5 us (level)
  no operation moved by 1% of the time
where the time goes in v6:
time: 31.5 us; the launch traced here: 31.4 us
  Pallas kernels  30.7 us (97%)
  between operations  0.64 us (2%)
    pallas_call x1, Pallas kernels, first(): pl.pallas_call(wide_kernel, out_shape=(jax.ShapeDtypeStruct((4, TILE, TIL...  27.8 us
    pallas_call x1, Pallas kernels, body(): pl.pallas_call(basis_kernel, out_shape=(jax.ShapeDtypeStruct((MODES, TILE...  2.96 us

profile of v6, /device:TPU:1, one launch (start us, length us, event | category | flops | bytes accessed | tf_op | source)
XLA Modules:
  0.0 31.4 jit_solution(15262438263699069924)
XLA Ops:
  0.6 27.8 %flow_and_gram.1 = (f32[4,128,128]{2,1,0:T(8,128)S(1)}, bf16[64,16384]{1,0:T(8,128)(2,1)S(1)}, f32[64,128]{1,0:T(8,128)S(1)}, f32[128,128]{1,0:T(8,128)S(1)}, f32[1,128]{1,0:T(1,128)S(1)}) custom-call(f32[4,128,128]{2,1,0:T(8,128)} %flow_hbm.1, f32[128,128]{1,0:T(8,128)} %sound_hbm.1, bf16[62,128,128]{2,1,0:T(8,128)(2,1)} %snap_hbm.1), custom_call_target="tpu_custom_call" | custom-call | tf_op jit(solution)/shard_map/flow_and_gram/pallas_call | solution.py:462
  28.4 3.0 %basis.1 = (f32[64,128,128]{2,1,0:T(8,128)}, f32[4,128,128]{2,1,0:T(8,128)}) custom-call(f32[64,128]{1,0:T(8,128)S(1)} %get-tuple-element.9.early_ref, f32[128,128]{1,0:T(8,128)S(1)} %get-tuple-element.10.normal_ref, f32[1,128]{1,0:T(1,128)S(1)} %get-tuple-element.11.late_ref, bf16[64,16384]{1,0:T(8,128)(2,1)S(1)} %get-tuple-element.12.block_ref, ...), custom_call_target="tpu_custom_call" | custom-call | tf_op jit(solution)/shard_map/basis/pallas_call | solution.py:511

commit v7 on v6

--- a/solution.py
+++ b/solution.py
@@ -14,7 +14,7 @@
 MODES = 64
 RESIDENT = 62
 TILE = 128
-EARLY_ROWS = 96
+EARLY_ROWS = 64
 HALO = 12
 PAD = 16
 ROWS = TILE + 2 * PAD

time: 31.5 us -> 31.4 us (level)
  no operation moved by 1% of the time
where the time goes in v7:
time: 31.4 us; the launch traced here: 31.3 us
  Pallas kernels  30.7 us (98%)
  between operations  0.64 us (2%)
    pallas_call x1, Pallas kernels, first(): pl.pallas_call(wide_kernel, out_shape=(jax.ShapeDtypeStruct((4, TILE, TIL...  27.7 us
    pallas_call x1, Pallas kernels, body(): pl.pallas_call(basis_kernel, out_shape=(jax.ShapeDtypeStruct((MODES, TILE...  2.96 us

profile of v7, /device:TPU:1, one launch (start us, length us, event | category | flops | bytes accessed | tf_op | source)
XLA Modules:
  0.0 31.3 jit_solution(18099718912568346013)
XLA Ops:
  0.6 27.7 %flow_and_gram.1 = (f32[4,128,128]{2,1,0:T(8,128)S(1)}, bf16[64,16384]{1,0:T(8,128)(2,1)S(1)}, f32[64,128]{1,0:T(8,128)S(1)}, f32[128,128]{1,0:T(8,128)S(1)}, f32[1,128]{1,0:T(1,128)S(1)}) custom-call(f32[4,128,128]{2,1,0:T(8,128)} %flow_hbm.1, f32[128,128]{1,0:T(8,128)} %sound_hbm.1, bf16[62,128,128]{2,1,0:T(8,128)(2,1)} %snap_hbm.1), custom_call_target="tpu_custom_call" | custom-call | tf_op jit(solution)/shard_map/flow_and_gram/pallas_call | solution.py:462
  28.4 3.0 %basis.1 = (f32[64,128,128]{2,1,0:T(8,128)}, f32[4,128,128]{2,1,0:T(8,128)}) custom-call(f32[64,128]{1,0:T(8,128)S(1)} %get-tuple-element.9.early_ref, f32[128,128]{1,0:T(8,128)S(1)} %get-tuple-element.10.normal_ref, f32[1,128]{1,0:T(1,128)S(1)} %get-tuple-element.11.late_ref, bf16[64,16384]{1,0:T(8,128)(2,1)S(1)} %get-tuple-element.12.block_ref, ...), custom_call_target="tpu_custom_call" | custom-call | tf_op jit(solution)/shard_map/basis/pallas_call | solution.py:511
